TPU v7x, 512 devices: a whole 4x4x16 slice. The times are simulated.
512 devices in a mesh: dp: 128 (over z_hi, y, x, core), tm: 4 (over z_lo).
Axes of the slice: x: 4, y: 4, z: 16 (z_hi: 4, z_lo: 4; z = z_hi * 4 + z_lo), core: 2. Of those that a mesh axis runs over, the one named last changes fastest.
Arguments:
- feats: bfloat16 [393216, 512], P(('dp', 'tm')), may hold values from -40 to 40, as said below
- codes: int32 [128, 2, 1536], P('dp', None, 'tm'), may hold values from 0 to 1023, as said below
- conv_weight: bfloat16 [2048, 512], replicated, may hold values from -0.125 to 0.125
- conv_bias: float32 [512], replicated, may hold values from -3 to 3
- proj_weight: bfloat16 [512, 256], replicated, may hold values from -0.25 to 0.25
- codebooks: bfloat16 [2, 1024, 256], replicated, may hold values from -4.1875 to 4.1875
Outputs:
- feat_grad: bfloat16 [393216, 512], P(('dp', 'tm'))
- conv_grad: float32 [2048, 512], P(('dp', 'tm'))
- bias_grad: float32 [512], replicated
- proj_grad: float32 [512, 256], replicated
- code_means: bfloat16 [2, 1024, 256], P(None, 'tm')
- code_usage: float32 [2, 1024], P(None, 'tm')
Inputs may be any that keep to these rules, and one draw needn't show every extreme that they name: `feats`: each clip has its own overall scale, and rows vary in scale within a clip. Codes are used with strongly unequal frequencies; on every level some codes occur in no frame.
All inputs are finite; a program needn't handle non-finite values.
Results may differ from a plain program's by a relative error of at most 0.0075.
Values may be sent and summed in bfloat16 or wider, within the bound.
A program may use at most 64 MiB of HBM per device.

v0:
```python
import jax
import jax.numpy as jnp
from jax import lax
from jax.sharding import PartitionSpec as P


def shifted(block, axis, distance):
    devices = range(lax.axis_size(axis))
    route = [(i - distance, i) for i in devices if i - distance in devices]
    return lax.ppermute(block, axis, route)


def own_codes(whole, per_shard):
    return lax.dynamic_slice_in_dim(whole, lax.axis_index("tm") * per_shard, per_shard, 1)


def shards(feats, codes, conv_weight, conv_bias, proj_weight, codebooks):
    frame_count = feats.shape[0] // 2
    channels = feats.shape[1]
    levels = codebooks.shape[0]
    book_size = codebooks.shape[1]
    devices_all = lax.axis_size("dp") * lax.axis_size("tm")
    total_frames = codes.shape[2] * devices_all
    per_shard = book_size // lax.axis_size("tm")
    left_rows = shifted(feats[-2:], "tm", 1)
    paired = jnp.concatenate([left_rows, feats], 0).reshape(frame_count + 1, 2 * channels)
    unfold = jnp.concatenate([paired[:-1], paired[1:]], 1)
    conv_out = jnp.dot(unfold, conv_weight, preferred_element_type=jnp.float32)
    hidden = (conv_out + conv_bias).astype(jnp.bfloat16)
    latent = jnp.dot(hidden, proj_weight, preferred_element_type=jnp.float32)
    residual = latent
    grad_total = jnp.zeros(latent.shape, jnp.float32)
    sums_list = []
    counts_list = []
    code_ids = lax.broadcasted_iota(jnp.int32, (1, book_size), 1)
    for level_index in range(levels):
        matches = codes[0, level_index][:, None] == code_ids
        onehot = matches.astype(jnp.float32)
        sums_list.append(jnp.dot(onehot.T, residual, precision=lax.Precision.HIGHEST))
        counts_list.append(jnp.sum(onehot, 0))
        chosen = jnp.dot(
            matches.astype(jnp.bfloat16), codebooks[level_index], preferred_element_type=jnp.float32
        )
        residual = residual - chosen
        grad_total = grad_total + residual
    local_sums = jnp.stack(sums_list)
    local_counts = jnp.stack(counts_list)
    latent_grad = grad_total.astype(jnp.bfloat16)
    proj_term = jnp.dot(hidden.T, latent_grad, preferred_element_type=jnp.float32)
    hidden_grad = jnp.dot(latent_grad, proj_weight.T, preferred_element_type=jnp.float32).astype(
        jnp.bfloat16
    )
    bias_term = jnp.sum(hidden_grad.astype(jnp.float32), 0)
    next_row = shifted(hidden_grad[:1], "tm", -1)
    extended = jnp.concatenate([hidden_grad, next_row], 0)
    grad_unfold = jnp.dot(extended, conv_weight.T, preferred_element_type=jnp.float32)
    grad_paired = grad_unfold[1:, : 2 * channels] + grad_unfold[:-1, 2 * channels :]
    feat_grad = grad_paired.reshape(2 * frame_count, channels).astype(jnp.bfloat16)
    proj_float = proj_weight.astype(jnp.float32)
    owned_corr = lax.psum_scatter(
        jnp.dot(unfold.T, latent_grad, preferred_element_type=jnp.float32),
        ("dp", "tm"),
        scatter_dimension=0,
        tiled=True,
    )
    conv_sum = jnp.dot(owned_corr, proj_float.T, precision=lax.Precision.HIGHEST)
    whole_sums, whole_counts, proj_sum, bias_sum = lax.psum(
        (local_sums, local_counts, proj_term, bias_term), ("dp", "tm")
    )
    code_sums = own_codes(whole_sums, per_shard)
    code_counts = own_codes(whole_counts, per_shard)
    conv_grad = conv_sum / total_frames
    proj_grad = proj_sum / total_frames
    bias_grad = bias_sum / total_frames
    code_means = (code_sums / jnp.maximum(code_counts, 1.0)[:, :, None]).astype(jnp.bfloat16)
    code_usage = code_counts * (book_size / total_frames)
    return (feat_grad, conv_grad, bias_grad, proj_grad, code_means, code_usage)


def solution(mesh):
    placed = (P(("dp", "tm"), None), P("dp", None, "tm"), P(), P(), P(), P())
    return jax.shard_map(
        shards,
        mesh=mesh,
        in_specs=placed,
        out_specs=(
            P(("dp", "tm"), None),
            P(("dp", "tm"), None),
            P(),
            P(),
            P(None, "tm", None),
            P(None, "tm"),
        ),
        check_vma=False,
    )
```

profile of v0, /device:TPU:1, one launch (start us, length us, event | category | flops | bytes accessed | tf_op | source)
XLA Modules:
  0.0 542.1 jit_solution(1550233877767440799)
XLA Ops:
  7.2 0.0 copy-start
  7.2 0.0 copy-start.1
  7.2 0.0 all-reduce.5.cloned.1.call-start
  7.2 0.9 slice.34
  8.1 4.3 collective-permute-start
  12.5 0.8 slice_reduce_fusion
  13.3 2.1 slice.37
  15.4 0.0 collective-permute-done
  15.4 0.0 copy-done.1
  15.4 1.1 pad_maximum_fusion.1
  16.4 0.0 copy-start.2
  16.4 2.2 slice.36
  18.6 0.0 copy-start.5
  18.6 1.2 constant_dynamic-update-slice_fusion.1
  19.8 0.0 copy-done.2
  19.9 0.1 constant_dynamic-update-slice_fusion
  19.9 0.0 copy-done
  19.9 0.0 copy-done.5
  19.9 0.0 copy-start.3
  20.0 1.0 fusion.7
  20.9 0.0 copy-done.3
  20.9 0.0 copy-start.4
  21.0 0.3 fusion.27
  21.2 1.5 fusion.5
  22.8 0.0 copy-done.4
  22.8 0.4 fusion.8
  23.2 1.5 fusion.6
  24.7 0.4 fusion.11
  25.2 1.1 fusion.29
  26.3 2.1 fusion.28
  28.4 1.5 pad_maximum_fusion
  29.9 0.0 all-reduce.5.cloned.1.call-update
  29.9 0.4 convert_reduce_fusion
  30.3 0.3 convert_reduce_fusion.2
  30.6 1.3 collective-permute-start.1
  31.9 111.7 %all-reduce.1 = (f32[512]{0:T(512)S(1)}, f32[2,1024]{1,0:T(2,128)S(1)}) all-reduce(f32[512]{0:T(512)S(1)} %get-tuple-element.15, f32[2,1024]{1,0:T(2,128)S(1)} %pad_maximum_fusion.2), channel_id=1, replica_groups=mesh['dp'=128,'tm'=4] {'dp','tm'}, use_global_device_ids=true, to_apply=%region_2.0 | all-reduce | flops 2560 | bytes 20480 | tf_op jit(solution)/shard_map/psum | solution.py:67
  143.6 0.6 broadcast_multiply_fusion.1
  144.2 0.6 dynamic-slice_multiply_fusion
  144.8 0.0 collective-permute-done.1
  144.8 1.0 fusion.20
  145.8 0.4 fusion
  146.2 1.1 convert_element_type.34
  147.3 382.5 %all-reduce.5.cloned.1.call-done = (f32[2048,256]{1,0:T(8,128)}, f32[512,256]{1,0:T(8,128)}, f32[2,1024,256]{2,1,0:T(8,128)}) async-done(((f32[2048,256]{1,0:T(8,128)}, f32[512,256]{1,0:T(8,128)}, f32[2,1024,256]{2,1,0:T(8,128)}), (f32[2048,256]{1,0:T(8,128)}, f32[512,256]{1,0:T(8,128)}, f32[2,1024,256]{2,1,0:T(8,128)})) %all-reduce.5.cloned.1.call-update) | async-done | bytes 4718608
  529.9 1.9 broadcast_multiply_fusion
  531.8 1.9 divide_convert_fusion
  533.7 1.6 convolution_multiply_fusion
  (2 shorter events, 0.0 us)
Async XLA Ops:
  7.2 12.8 %copy-start = (bf16[2048,512]{1,0:T(8,128)(2,1)S(1)}, bf16[2048,512]{1,0:T(8,128)(2,1)}, u32[]{:S(2)}) copy-start(bf16[2048,512]{1,0:T(8,128)(2,1)} %param.8) | copy-start | bytes 6291460
  7.2 8.2 %copy-start.1 = (bf16[768,512]{1,0:T(8,128)(2,1)S(1)}, bf16[768,512]{1,0:T(8,128)(2,1)}, u32[]{:S(2)}) copy-start(bf16[768,512]{1,0:T(8,128)(2,1)} %param.6) | copy-start | bytes 2359300
  7.2 522.7 %all-reduce.5.cloned.1.call-start = ((), (), s32[]{:S(2)}) async-start(), calls=%async_computation | async-start | bytes 9437184
  8.1 7.2 %collective-permute-start = (bf16[2,512]{1,0:T(2,128)(2,1)S(1)}, bf16[2,512]{1,0:T(2,128)(2,1)S(1)}, u32[]{:S(2)}, u32[]{:S(2)}) collective-permute-start(bf16[2,512]{1,0:T(2,128)(2,1)S(1)} %slice.34), channel_id=1, source_target_pairs={{0,1},{1,2},{2,3},{4,5},{5,6},{6,7},{8,9},{9,10},{10,11},{12,13},{... | collective-permute-start | bytes 6152 | tf_op jit(solution)/shard_map/ppermute | solution.py:10
  16.4 3.4 copy-start.2
  18.6 1.3 copy-start.5
  19.9 1.0 copy-start.3
  20.9 1.8 copy-start.4
  30.6 114.2 %collective-permute-start.1 = (bf16[1,512]{1,0:T(2,128)(2,1)S(1)}, bf16[1,512]{1,0:T(2,128)(2,1)S(1)}, u32[]{:S(2)}, u32[]{:S(2)}) collective-permute-start(bf16[1,512]{1,0:T(2,128)(2,1)S(1)} %slice.45), channel_id=1, source_target_pairs={{1,0},{2,1},{3,2},{5,4},{6,5},{7,6},{9,8},{10,9},{11,10},{13,12},{... | collective-permute-start | bytes 3080 | tf_op jit(solution)/shard_map/ppermute | solution.py:10
Sparse Core Ops, SparseCore 0:
  30.0 499.8 all-reduce.4
where the time goes:
time: 543 us; the launch traced here: 542 us
  waiting for transfers between devices  383 us (71%)
  blocking collectives  112 us (21%)
  between operations  14.2 us (3%)
  matrix products  11.3 us (2%)
  local copies, waits for them, and re-layouts  8.41 us (2%)
  other arithmetic  8.23 us (2%)
  starting transfers between devices  5.68 us (1%)
    unnamed x2, waiting for transfers between devices  383 us
    psum x1, blocking collectives, shards(): lax.psum((local_sums, local_counts, proj_term, bias_term), ('dp', 'tm'))  112 us
  transfers between devices with their start and end apart: 3, of which 1 were waited for; matrix products, arithmetic and copies ran while one was open for 1% of the time, Pallas kernels for 0%

commit v1 on v0

v1 whole, which is shorter than its diff:
```python
import functools

import jax
import jax.numpy as jnp
from jax import lax
from jax.experimental import pallas as pl
from jax.experimental.pallas import tpu as pltpu
from jax.sharding import PartitionSpec as P

MESH = pl.DeviceIdType.MESH
BF = jnp.bfloat16
F32 = jnp.float32
NC = 2


def dot(a, b, ca=1, cb=0):
    return lax.dot_general(a, b, (((ca,), (cb,)), ((), ())), preferred_element_type=F32)


class Sems:
    def __init__(self, send, recv):
        self.send, self.recv, self.count, self.started, self.index = send, recv, 0, [], {}

    def copy(self, src, dst, device):
        index = self.count
        self.count += 1
        made = pltpu.make_async_remote_copy(
            src_ref=src, dst_ref=dst, send_sem=self.send.at[index], recv_sem=self.recv.at[index],
            device_id=device, device_id_type=MESH,
        )
        self.index[id(made)] = index
        return made

    def arrived(self, made, ref, device):
        index = self.index[id(made)]
        pltpu.make_async_remote_copy(
            src_ref=ref, dst_ref=ref, send_sem=self.send.at[index], recv_sem=self.recv.at[index],
            device_id=device, device_id_type=MESH,
        ).wait_recv()

    def start(self, src, dst, device):
        made = self.copy(src, dst, device)
        made.start()
        self.started.append(made)
        return made


def kernel(g, feats, codes, conv_w, conv_b, proj_w, books,
           fg_out, conv_out, bias_out, proj_out, means_out, usage_out,
           feats_v, cw_v, pw_v, books_v, fx, unf, acc_v, hid, lat, lg_v, hgf, halo_v, next_v, fg_f, fg_v,
           s0_0, s0_c, s0_1, s0_r1, s0_2, s0_r2,
           s1_0, s1_c, s1_1, s1_r1, s1_2, s1_r2,
           pr_0, pr_c, pr_1, pr_r1, pr_2, pr_r2,
           ca_0, ca_c, ca_1, ca_r1, ca_2, ca_r2,
           cb_0, cb_c, cb_1, cb_r1, cb_2, cb_r2,
           sm_c, sm_x, sm_y, sm_l, sm_h, sm_f,
           zl_s, zl_r, zh_r, ch_s, ch_r, cl_r, conv_f, ag_s, ag_p,
           in_sem, out_sem, send_sem, recv_sem):
    nx, ny, zh_n, zl_n = g["nx"], g["ny"], g["zh"], g["zl"]
    frames, chan, dz, book = g["frames"], g["chan"], g["dz"], g["book"]
    total = g["total"]
    rs, rp, rpd = g["rs"], g["rp"], g["rpd"]
    tile = zl_n * rpd
    zhh = zh_n // 2
    lanes = chan // 128

    dp, zl = lax.axis_index("dp"), lax.axis_index("tm")
    c = dp % NC
    x = dp // NC % nx
    y = dp // (NC * nx) % ny
    zh = dp // (NC * nx * ny)

    def dev(c_, x_, y_, zh_, zl_):
        return (((zh_ * ny + y_) * nx + x_) * NC + c_, zl_)

    def at_core():
        return dev(1 - c, x, y, zh, zl)

    def at_x(d):
        return dev(c, (x + d) % nx, y, zh, zl)

    def at_y(d):
        return dev(c, x, (y + d) % ny, zh, zl)

    def at_l(d):
        return dev(c, x, y, zh, (zl + d) % zl_n)

    def at_h(d):
        return dev(c, x, y, (zh + d) % zh_n, zl)

    sems = Sems(send_sem, recv_sem)

    barrier = pltpu.get_barrier_semaphore()
    partners = [at_core()]
    for ring, n in ((at_x, nx), (at_y, ny), (at_l, zl_n), (at_h, zh_n)):
        partners += [ring(d) for d in range(1, n)]
    for partner in partners:
        pl.semaphore_signal(barrier, inc=1, device_id=partner, device_id_type=MESH)

    half = 2 * chan
    loads = [
        pltpu.make_async_copy(feats, feats_v, in_sem.at[0]),
        pltpu.make_async_copy(conv_w.at[pl.ds(half, half)], cw_v.at[pl.ds(half, half)], in_sem.at[1]),
        pltpu.make_async_copy(conv_w.at[pl.ds(0, half)], cw_v.at[pl.ds(0, half)], in_sem.at[2]),
        pltpu.make_async_copy(proj_w, pw_v, in_sem.at[3]),
        pltpu.make_async_copy(books, books_v, in_sem.at[4]),
    ]
    for load in loads:
        load.start()

    rows_in = 2 * frames
    loads[0].wait()
    for k in range(lanes):
        fx[k, pl.ds(8, rows_in), :] = feats_v[:, k * 128:(k + 1) * 128].astype(F32)

    def spread(start, tap):
        for k in range(lanes):
            piece = fx[k, pl.ds(start, frames, stride=2), :]
            unf[:, tap * chan + k * 128:tap * chan + (k + 1) * 128] = piece.astype(BF)

    spread(8, 2)
    spread(9, 3)
    loads[1].wait()
    acc_v[...] = dot(unf[:, half:], cw_v[half:, :])

    pl.semaphore_wait(barrier, len(partners))
    halo = sems.copy(feats_v.at[pl.ds(rows_in - 16, 16)], halo_v, at_l(1))

    @pl.when(zl < zl_n - 1)
    def _():
        halo.start()

    code_rows = codes[0].astype(F32)
    lane_ids = lax.broadcasted_iota(jnp.int32, (frames, book), 1).astype(F32)

    def onehot(level):
        eye = (lax.broadcasted_iota(jnp.int32, (frames, frames), 0)
               == lax.broadcasted_iota(jnp.int32, (frames, frames), 1))
        column = jnp.sum(jnp.where(eye, code_rows[level:level + 1, :], 0.0), 1, keepdims=True)
        return (column == lane_ids).astype(F32)

    per_q = book // zl_n
    per_c = nx * ny * rs

    def onehot_t(level, side):
        rows = nx * ny * zl_n * rs
        p = lax.broadcasted_iota(jnp.int32, (rows, 1), 0)
        i = p % rs
        q = p // rs % zl_n
        if level == 0:
            yy = p // (rs * zl_n) % ny
            xx = p // (rs * zl_n * ny)
        else:
            xx = p // (rs * zl_n) % nx
            yy = p // (rs * zl_n * nx)
        ids = q * per_q + side * per_c + (xx * ny + yy) * rs + i
        return (ids.astype(F32) == code_rows[level:level + 1, :]).astype(F32).astype(BF)

    small_rows = book // 128
    oh0 = onehot(0)
    oh1 = onehot(1)
    for level, oh in enumerate((oh0, oh1)):
        count = jnp.sum(oh, 0, keepdims=True)
        for r in range(small_rows):
            sm_c[0, pl.ds(level * small_rows + r, 1), :] = count[:, r * 128:(r + 1) * 128]

    @pl.when(zl == 0)
    def _():
        halo_v[...] = jnp.zeros(halo_v.shape, BF)

    @pl.when(zl > 0)
    def _():
        halo.wait_recv()

    last = halo_v[...].astype(F32)[8:16, :]
    for k in range(lanes):
        fx[k, pl.ds(0, 8), :] = last[:, k * 128:(k + 1) * 128]
    spread(6, 0)
    spread(7, 1)
    loads[2].wait()
    conv = acc_v[...] + dot(unf[:, :half], cw_v[:half, :])
    hid[...] = (conv + conv_b[...]).astype(BF)
    loads[3].wait()
    lat[...] = dot(hid[...], pw_v[...])

    def level_sums(level, ref0, refc):
        value = lat[...]
        hi = value.astype(BF)
        lo = (value - hi.astype(F32)).astype(BF)

        def part(side):
            oh = onehot_t(level, side)
            made = dot(oh, hi) + dot(oh, lo)
            ref0[side] = made.astype(BF).reshape(ref0.shape[1:])

        part(1 - c)
        copy = sems.start(ref0.at[1 - c], refc, at_core())
        part(c)
        return copy

    s0_core = level_sums(0, s0_0, s0_c)
    loads[4].wait()
    r1 = lat[...] - dot(oh0.astype(BF), books_v[0])
    lat[...] = r1
    s1_core = level_sums(1, s1_0, s1_c)

    def stage1(core_copy, ref0, refc, ref1, refr, ring, n, me):
        core_copy.wait_recv()
        ref1[...] = (ref0[c].astype(F32) + refc[...].astype(F32)).astype(BF)
        return [sems.start(ref1.at[(me + d) % n], refr.at[d - 1], ring(d)) for d in range(1, n)]

    def stage2(copies, ref1, refr, ref2, refr2, ring, n, me, me1):
        made = ref1[me1].astype(F32)
        for d, copy in enumerate(copies):
            copy.wait_recv()
            made = made + refr[d].astype(F32)
        ref2[...] = made.astype(BF).reshape(ref2.shape)
        return [sems.start(ref2.at[(me + d) % n], refr2.at[d - 1], ring(d)) for d in range(1, n)]

    def finish(copies, ref2, refr2, me):
        made = ref2[me].astype(F32)
        for d, copy in enumerate(copies):
            copy.wait_recv()
            made = made + refr2[d].astype(F32)
        return made

    s0_x = stage1(s0_core, s0_0, s0_c, s0_1, s0_r1, at_x, nx, x)

    value = lat[...]
    lg = (value + (value - dot(oh1.astype(BF), books_v[1]))).astype(BF)
    lg_v[...] = lg
    pr_0[...] = dot(hid[...], lg, 0, 0).astype(BF).reshape(pr_0.shape)
    pr_core = sems.start(pr_0.at[1 - c], pr_c, at_core())

    s1_y = stage1(s1_core, s1_0, s1_c, s1_1, s1_r1, at_y, ny, y)

    hg = dot(lg, pw_v[...], 1, 1).astype(BF)
    hid[...] = hg
    hgw = hg.astype(F32)
    hgf[pl.ds(0, frames), :] = hgw
    nxt = sems.copy(hid.at[pl.ds(0, 16)], next_v, at_l(-1 + zl_n))

    @pl.when(zl > 0)
    def _():
        nxt.start()

    bias = jnp.sum(hgw, 0, keepdims=True)
    for r in range(lanes):
        sm_c[0, pl.ds(2 * small_rows + r, 1), :] = bias[:, r * 128:(r + 1) * 128]
    pad = sm_c.shape[1] - 2 * small_rows - lanes
    if pad:
        sm_c[0, pl.ds(2 * small_rows + lanes, pad), :] = jnp.zeros((pad, 128), F32)
    sm_core = sems.start(sm_c.at[0], sm_c.at[1], at_core())

    def corr(base, ref0, x_first):
        group = nx * NC * tile
        for zz in range(zhh):
            for yy in range(ny):
                start = base + (zz * ny + yy) * group
                made = dot(unf[:, start:start + group], lg_v[...], 0, 0).astype(BF)
                for xx in range(nx):
                    for cc in range(NC):
                        at = (xx * NC + cc) * tile
                        a, b = (xx, yy) if x_first else (yy, xx)
                        row = (b * zhh + zz) * tile
                        ref0[cc, a, row:row + tile, :] = made[at:at + tile, :]

    corr(0, ca_0, True)
    ca_core = sems.start(ca_0.at[1 - c], ca_c, at_core())
    pr_x = stage1(pr_core, pr_0, pr_c, pr_1, pr_r1, at_x, nx, x)
    corr(half, cb_0, False)
    cb_core = sems.start(cb_0.at[1 - c], cb_c, at_core())

    def small(copies, ref, me, n, nxt_ref):
        for copy in copies:
            copy.wait_recv()
        made = None
        for j in range(n):
            piece = ref[(me - j + n) % n]
            made = piece if made is None else made + piece
        nxt_ref[...] = made

    def small_send(ref, ring, n):
        return [sems.start(ref.at[0], ref.at[d], ring(d)) for d in range(1, n)]

    small([sm_core], sm_c, c, NC, sm_x.at[0])
    sm_xs = small_send(sm_x, at_x, nx)

    s0_y = stage2(s0_x, s0_1, s0_r1, s0_2, s0_r2, at_y, ny, y, x)
    s1_x = stage2(s1_y, s1_1, s1_r1, s1_2, s1_r2, at_x, nx, x, y)
    pr_y = stage2(pr_x, pr_1, pr_r1, pr_2, pr_r2, at_y, ny, y, x)
    small(sm_xs, sm_x, x, nx, sm_y.at[0])
    sm_ys = small_send(sm_y, at_y, ny)
    ca_x = stage1(ca_core, ca_0, ca_c, ca_1, ca_r1, at_x, nx, x)
    cb_y = stage1(cb_core, cb_0, cb_c, cb_1, cb_r1, at_y, ny, y)

    s0_d = finish(s0_y, s0_2, s0_r2, y)
    s1_d = finish(s1_x, s1_2, s1_r2, x)
    pr_d = finish(pr_y, pr_2, pr_r2, y)
    for q in range(zl_n):
        zl_s[q] = jnp.concatenate(
            [s0_d[q * rs:(q + 1) * rs], s1_d[q * rs:(q + 1) * rs], pr_d], 0).astype(BF)
    zl_c = [sems.start(zl_s.at[(zl + d) % zl_n], zl_r.at[d], at_l(d)) for d in range(1, zl_n)]
    zl_r[0] = zl_s[zl]
    small(sm_ys, sm_y, y, ny, sm_l.at[0])
    sm_ls = small_send(sm_l, at_l, zl_n)

    @pl.when(zl == zl_n - 1)
    def _():
        next_v[...] = jnp.zeros(next_v.shape, BF)

    @pl.when(zl < zl_n - 1)
    def _():
        nxt.wait_recv()

    hgf[pl.ds(frames, 8), :] = next_v[...].astype(F32)[0:8, :]
    lg_next = hgf[pl.ds(1, frames), :].astype(BF)

    def feat_part(part):
        made = (dot(lg_next, cw_v[pl.ds(part * chan, chan), :], 1, 1)
                + dot(hid[...], cw_v[pl.ds(half + part * chan, chan), :], 1, 1))
        for k in range(lanes):
            fg_f[k, pl.ds(part, frames, stride=2), :] = made[:, k * 128:(k + 1) * 128]

    feat_part(0)
    feat_part(1)

    def summed(copies, ref, me, n):
        for copy in copies:
            copy.wait_recv()
        made = None
        for j in range(n):
            piece = ref[(me - j + n) % n].astype(F32)
            made = piece if made is None else made + piece
        return made

    zh_r[0] = summed(zl_c, zl_r, zl, zl_n).astype(BF)
    zh_c = [sems.start(zh_r.at[0], zh_r.at[d], at_h(d)) for d in range(1, zh_n)]
    small(sm_ls, sm_l, zl, zl_n, sm_h.at[0])
    sm_hs = small_send(sm_h, at_h, zh_n)

    ca_y = stage2(ca_x, ca_1, ca_r1, ca_2, ca_r2, at_y, ny, y, x)
    cb_x = stage2(cb_y, cb_1, cb_r1, cb_2, cb_r2, at_x, nx, x, y)

    for k in range(lanes):
        fg_v[:, k * 128:(k + 1) * 128] = fg_f[k].astype(BF)
    fg_store = pltpu.make_async_copy(fg_v, fg_out, out_sem.at[0])
    fg_store.start()

    ca_d = finish(ca_y, ca_2, ca_r2, y)
    cb_d = finish(cb_x, cb_2, cb_r2, x)
    for zz in range(zhh):
        ch_s[zz] = ca_d[zz * tile:(zz + 1) * tile].astype(BF)
        ch_s[zhh + zz] = cb_d[zz * tile:(zz + 1) * tile].astype(BF)
    ch_c = [sems.start(ch_s.at[(zh + d) % zh_n], ch_r.at[d], at_h(d)) for d in range(1, zh_n)]
    ch_r[0] = ch_s[zh]

    small(sm_hs, sm_h, zh, zh_n, sm_f)
    q_rows = per_q // 128
    base = c * per_c + (x * ny + y) * rs
    ids = lax.broadcasted_iota(jnp.int32, (rs, 128), 1) - lax.broadcasted_iota(jnp.int32, (rs, 128), 0)
    columns = []
    for level in range(2):
        row = sm_f[pl.ds(level * small_rows + zl * q_rows + base // 128, 1), :]
        columns.append(jnp.sum(jnp.where(ids == base % 128, row, 0.0), 1, keepdims=True))
        for r in range(q_rows):
            count = sm_f[pl.ds(level * small_rows + zl * q_rows + r, 1), :]
            usage_out[level:level + 1, r * 128:(r + 1) * 128] = count * (book / total)
    for r in range(lanes):
        bias_out[:, r * 128:(r + 1) * 128] = sm_f[2 * small_rows + r:2 * small_rows + r + 1, :] / total
    counts = jnp.maximum(jnp.concatenate(columns, 0), 1.0)

    done = summed(zh_c, zh_r, zh, zh_n)
    ag_s[c, x, y] = (done[:2 * rs] / counts).astype(BF)
    ag_p[c, y, x] = done[2 * rs:].astype(BF)
    gs = [sems.start(ag_s.at[c, x, y], ag_s.at[c, x, y], at_y(d)) for d in range(1, ny)]
    gp = [sems.start(ag_p.at[c, y, x], ag_p.at[c, y, x], at_x(d)) for d in range(1, nx)]

    def gathered(sem_copies, ref_of, n, me):
        for d, copy in enumerate(sem_copies):
            src = (me - (d + 1) + n) % n
            sems.arrived(copy, ref_of(src), at_core())

    gathered(gs, lambda j: ag_s.at[c, x, j], ny, y)
    gs2 = [sems.start(ag_s.at[c, x], ag_s.at[c, x], at_x(d)) for d in range(1, nx)]
    gathered(gp, lambda j: ag_p.at[c, y, j], nx, x)
    gp2 = [sems.start(ag_p.at[c, y], ag_p.at[c, y], at_y(d)) for d in range(1, ny)]

    cl_r[0] = summed(ch_c, ch_r, zh, zh_n).astype(BF)
    cl_c = [sems.start(cl_r.at[0], cl_r.at[d], at_l(d)) for d in range(1, zl_n)]

    gathered(gs2, lambda j: ag_s.at[c, j], nx, x)
    gs3 = sems.start(ag_s.at[c], ag_s.at[c], at_core())
    gathered(gp2, lambda j: ag_p.at[c, j], ny, y)
    gp3 = sems.start(ag_p.at[c], ag_p.at[c], at_core())

    owned = summed(cl_c, cl_r, zl, zl_n)
    top = owned.astype(BF)
    low = (owned - top.astype(F32)).astype(BF)
    made = (dot(top, pw_v[...], 1, 1) + dot(low, pw_v[...], 1, 1)) / total
    conv_f[...] = made
    picked = None
    for q in range(zl_n):
        piece = jnp.where(zl == q, conv_f[q * rpd:(q + 1) * rpd, :], 0.0)
        picked = piece if picked is None else picked + piece
    conv_out[...] = picked

    gathered([gs3], lambda j: ag_s.at[1 - c], 1, 0)
    for cc in range(NC):
        for xx in range(nx):
            for level in range(2):
                rows = [ag_s[cc, xx, yy].astype(F32)[level * rs:(level + 1) * rs] for yy in range(ny)]
                at = cc * per_c + xx * ny * rs
                means_out[level, at:at + ny * rs, :] = jnp.concatenate(rows, 0).astype(BF)
    gathered([gp3], lambda j: ag_p.at[1 - c], 1, 0)
    for cc in range(NC):
        for xx in range(nx):
            for yy in range(ny):
                at = ((cc * nx + xx) * ny + yy) * rp
                proj_out[at:at + rp, :] = ag_p[cc, yy, xx].astype(F32) * (1.0 / total)

    fg_store.wait()
    for copy in sems.started:
        copy.wait_send()

    @pl.when(zl < zl_n - 1)
    def _():
        halo.wait_send()

    @pl.when(zl > 0)
    def _():
        nxt.wait_send()


def shards(g, feats, codes, conv_weight, conv_bias, proj_weight, codebooks):
    rows_in, chan = feats.shape
    frames = rows_in // 2
    dz = proj_weight.shape[1]
    book = codebooks.shape[1]
    nx, ny, zhn, zln = g["nx"], g["ny"], g["zh"], g["zl"]
    devices = NC * nx * ny * zhn * zln
    taps = conv_weight.shape[0]
    g = dict(g, frames=frames, chan=chan, dz=dz, book=book, total=float(frames * devices),
             rs=book // (NC * nx * ny * zln), rp=chan // (NC * nx * ny), rpd=taps // devices)
    rs, rp, rpd = g["rs"], g["rp"], g["rpd"]
    tile = zln * rpd
    lanes = chan // 128

    def flow(a, b, rows):
        return [
            pltpu.VMEM((NC, a, b * rows, dz), BF),
            pltpu.VMEM((a, b * rows, dz), BF),
            pltpu.VMEM((a, b * rows, dz), BF),
            pltpu.VMEM((max(a - 1, 1), b * rows, dz), BF),
            pltpu.VMEM((b, rows, dz), BF),
            pltpu.VMEM((max(b - 1, 1), rows, dz), BF),
        ]

    small = -(-(2 * book // 128 + lanes) // 8) * 8
    zrows = 2 * rs + rp
    scratch = [
        pltpu.VMEM((rows_in, chan), BF),
        pltpu.VMEM((taps, chan), BF),
        pltpu.VMEM((chan, dz), BF),
        pltpu.VMEM((2, book, dz), BF),
        pltpu.VMEM((lanes, rows_in + 8, 128), F32),
        pltpu.VMEM((frames, taps), BF),
        pltpu.VMEM((frames, chan), F32),
        pltpu.VMEM((frames, chan), BF),
        pltpu.VMEM((frames, dz), F32),
        pltpu.VMEM((frames, dz), BF),
        pltpu.VMEM((frames + 8, chan), F32),
        pltpu.VMEM((16, chan), BF),
        pltpu.VMEM((16, chan), BF),
        pltpu.VMEM((lanes, rows_in, 128), F32),
        pltpu.VMEM((rows_in, chan), BF),
    ]
    scratch += flow(nx, ny, zln * rs)
    scratch += flow(ny, nx, zln * rs)
    scratch += flow(nx, ny, rp)
    scratch += flow(nx, ny, zhn // 2 * tile)
    scratch += flow(ny, nx, zhn // 2 * tile)
    scratch += [pltpu.VMEM((n, small, 128), F32) for n in (NC, nx, ny, zln, zhn)]
    scratch += [
        pltpu.VMEM((small, 128), F32),
        pltpu.VMEM((zln, zrows, dz), BF),
        pltpu.VMEM((zln, zrows, dz), BF),
        pltpu.VMEM((zhn, zrows, dz), BF),
        pltpu.VMEM((zhn, tile, dz), BF),
        pltpu.VMEM((zhn, tile, dz), BF),
        pltpu.VMEM((zln, tile, dz), BF),
        pltpu.VMEM((tile, chan), F32),
        pltpu.VMEM((NC, nx, ny, 2 * rs, dz), BF),
        pltpu.VMEM((NC, ny, nx, rp, dz), BF),
        pltpu.SemaphoreType.DMA((5,)),
        pltpu.SemaphoreType.DMA((1,)),
        pltpu.SemaphoreType.DMA((96,)),
        pltpu.SemaphoreType.DMA((96,)),
    ]
    any_spec = pl.BlockSpec(memory_space=pl.ANY)
    vmem = pl.BlockSpec(memory_space=pltpu.VMEM)
    out = pl.pallas_call(
        functools.partial(kernel, g),
        out_shape=(
            jax.ShapeDtypeStruct((rows_in, chan), BF),
            jax.ShapeDtypeStruct((rpd, chan), F32),
            jax.ShapeDtypeStruct((1, chan), F32),
            jax.ShapeDtypeStruct((chan, dz), F32),
            jax.ShapeDtypeStruct((2, book // zln, dz), BF),
            jax.ShapeDtypeStruct((2, book // zln), F32),
        ),
        in_specs=[any_spec, vmem, any_spec, vmem, any_spec, any_spec],
        out_specs=(any_spec, vmem, vmem, vmem, vmem, vmem),
        scratch_shapes=scratch,
        compiler_params=pltpu.CompilerParams(
            collective_id=0, has_side_effects=True, vmem_limit_bytes=56 << 20),
    )(feats, codes, conv_weight, conv_bias.reshape(1, chan), proj_weight, codebooks)
    fg, cg, bg, pg, cm, cu = out
    return fg, cg, bg.reshape(chan), pg, cm, cu


def solution(mesh, g=None):
    if g is None:
        g = {"nx": 4, "ny": 4, "zh": 4, "zl": 4}
    placed = (P(("dp", "tm"), None), P("dp", None, "tm"), P(), P(), P(), P())
    return jax.shard_map(
        functools.partial(shards, g),
        mesh=mesh,
        in_specs=placed,
        out_specs=(
            P(("dp", "tm"), None),
            P(("dp", "tm"), None),
            P(),
            P(),
            P(None, "tm", None),
            P(None, "tm"),
        ),
        check_vma=False,
    )
```

time: 543 us -> 68.1 us (0.13)
  waiting for transfers between devices: 383 us -> 0 us
  blocking collectives: 112 us -> 0 us
  Pallas kernels: 0 us -> 59.4 us
  between operations: 14.2 us -> 0.66 us
  matrix products: 11.3 us -> 0 us
  other arithmetic: 8.23 us -> 0 us
  starting transfers between devices: 5.68 us -> 0 us
    unnamed x2 -> x0, waiting for transfers between devices: 383 us -> none
    psum x1 -> x0, blocking collectives: 112 us -> none  [shards(): lax.psum((local_sums, local_counts, proj_term, bias_term), ('dp', 'tm'))]
    pallas_call x0 -> x1, Pallas kernels: none -> 59.4 us  [shards(): pl.pallas_call(functools.partial(kernel, g), out_shape=(jax.ShapeDtypeStr...]
    dot_general x11 -> x0, matrix products: 11.3 us -> none  [the longest x2 3.06 us: shards(): jnp.dot(onehot.T, residual, precision=lax.Precision.HIGHEST)]
    unnamed x13 -> x10, local copies, waits for them, and re-layouts: 1.24 us -> 7.81 us
    slice x5 -> x0, local copies, waits for them, and re-layouts: 5.97 us -> none  [the longest x2 4.31 us: shards(): unfold = jnp.concatenate([paired[:-1], paired[1:]], 1)]
    ppermute x2 -> x0, starting transfers between devices: 5.64 us -> none  [shifted(): return lax.ppermute(block, axis, route)]
  transfers between devices with their start and end apart: 3 -> 0, of which waited for: 1 -> 0; matrix products, arithmetic and copies ran while one was open for 1% -> 0% of each run, Pallas kernels for 0% -> 0%
where the time goes in v1:
time: 68.1 us; the launch traced here: 67.8 us
  Pallas kernels  59.4 us (87%)
  local copies, waits for them, and re-layouts  7.81 us (11%)
    pallas_call x1, Pallas kernels, shards(): pl.pallas_call(functools.partial(kernel, g), out_shape=(jax.ShapeDtypeStr...  59.4 us
    unnamed x10, local copies, waits for them, and re-layouts  7.81 us

profile of v1, /device:TPU:1, one launch (start us, length us, event | category | flops | bytes accessed | tf_op | source)
XLA Modules:
  0.0 67.8 jit_solution(10737529478406793126)
XLA Ops:
  0.6 59.4 %shard_map.109 = (bf16[768,512]{1,0:T(8,128)(2,1)}, f32[4,512]{1,0:T(4,128)}, f32[1,512]{1,0:T(1,128)}, f32[512,256]{1,0:T(8,128)}, bf16[2,256,256]{2,1,0:T(8,128)(2,1)}, /*index=5*/f32[2,256]{1,0:T(2,128)}) custom-call(bf16[768,512]{1,0:T(8,128)(2,1)} %feats.1, s32[1,2,384]{2,1,0:T(2,128)} %codes.1, bf16[2048,512]{1,0:T(8,128)(2,1)} %conv_w.1, ...), custom_call_target="tpu_custom_call" | custom-call | tf_op jit(solution)/shard_map/pallas_call | solution.py:502
  60.0 0.0 copy-start
  60.0 0.0 copy-start.1
  60.0 2.1 %copy.18 = bf16[768,512]{1,0:T(8,128)(2,1)} copy(bf16[768,512]{1,0:T(8,128)(2,1)} %get-tuple-element.24) | data formatting | bytes 1572864
  62.1 1.3 %copy.19 = f32[4,512]{1,0:T(4,128)} copy(f32[4,512]{1,0:T(4,128)} %get-tuple-element.25) | data formatting | bytes 16384
  63.4 1.3 %copy.20 = f32[512]{0:T(512)} copy(f32[512]{0:T(512)} %bitcast.3) | data formatting | bytes 4096
  64.7 1.9 %copy.21 = f32[512,256]{1,0:T(8,128)} copy(f32[512,256]{1,0:T(8,128)} %get-tuple-element.27) | data formatting | bytes 1048576
  66.5 0.0 copy-done
  66.5 0.7 %copy.22 = bf16[2,256,256]{2,1,0:T(8,128)(2,1)} copy(bf16[2,256,256]{2,1,0:T(8,128)(2,1)S(1)} %copy-done) | data formatting | bytes 524288
  67.2 0.0 copy-done.1
  67.2 0.6 copy.23
Async XLA Ops:
  60.0 6.5 %copy-start = (bf16[2,256,256]{2,1,0:T(8,128)(2,1)S(1)}, bf16[2,256,256]{2,1,0:T(8,128)(2,1)}, u32[]{:S(2)}) copy-start(bf16[2,256,256]{2,1,0:T(8,128)(2,1)} %get-tuple-element.28) | copy-start | bytes 786436
  60.0 7.2 %copy-start.1 = (f32[2,256]{1,0:T(2,128)S(1)}, f32[2,256]{1,0:T(2,128)}, u32[]{:S(2)}) copy-start(f32[2,256]{1,0:T(2,128)} %get-tuple-element.29) | copy-start | bytes 6148

commit v2 on v1

--- a/solution.py
+++ b/solution.py
@@ -45,17 +45,17 @@
         return made
 
 
-def kernel(g, feats, codes, conv_w, conv_b, proj_w, books,
-           fg_out, conv_out, bias_out, proj_out, means_out, usage_out,
-           feats_v, cw_v, pw_v, books_v, fx, unf, acc_v, hid, lat, lg_v, hgf, halo_v, next_v, fg_f, fg_v,
+def kernel(g, feats, codes_in, conv_w, conv_b_in, proj_w, books,
+           fg_out, conv_f, sm_f, ag_s, ag_p,
+           feats_v, codes, cw_v, conv_b, pw_v, books_v, oh_v, fx, unf, acc_v, hid, lat, lg_v, hgf, halo_v, next_v, fg_f,
            s0_0, s0_c, s0_1, s0_r1, s0_2, s0_r2,
            s1_0, s1_c, s1_1, s1_r1, s1_2, s1_r2,
            pr_0, pr_c, pr_1, pr_r1, pr_2, pr_r2,
            ca_0, ca_c, ca_1, ca_r1, ca_2, ca_r2,
            cb_0, cb_c, cb_1, cb_r1, cb_2, cb_r2,
-           sm_c, sm_x, sm_y, sm_l, sm_h, sm_f,
-           zl_s, zl_r, zh_r, ch_s, ch_r, cl_r, conv_f, ag_s, ag_p,
-           in_sem, out_sem, send_sem, recv_sem):
+           sm_c, sm_x, sm_y, sm_l, sm_h,
+           zl_s, zl_r, zh_r, ch_s, ch_r, cl_r,
+           in_sem, send_sem, recv_sem):
     nx, ny, zh_n, zl_n = g["nx"], g["ny"], g["zh"], g["zl"]
     frames, chan, dz, book = g["frames"], g["chan"], g["dz"], g["book"]
     total = g["total"]
@@ -104,6 +104,8 @@
         pltpu.make_async_copy(conv_w.at[pl.ds(0, half)], cw_v.at[pl.ds(0, half)], in_sem.at[2]),
         pltpu.make_async_copy(proj_w, pw_v, in_sem.at[3]),
         pltpu.make_async_copy(books, books_v, in_sem.at[4]),
+        pltpu.make_async_copy(codes_in, codes, in_sem.at[5]),
+        pltpu.make_async_copy(conv_b_in, conv_b, in_sem.at[6]),
     ]
     for load in loads:
         load.start()
@@ -130,14 +132,17 @@
     def _():
         halo.start()
 
-    code_rows = codes[0].astype(F32)
-    lane_ids = lax.broadcasted_iota(jnp.int32, (frames, book), 1).astype(F32)
+    small_rows = book // 128
 
     def onehot(level):
         eye = (lax.broadcasted_iota(jnp.int32, (frames, frames), 0)
                == lax.broadcasted_iota(jnp.int32, (frames, frames), 1))
         column = jnp.sum(jnp.where(eye, code_rows[level:level + 1, :], 0.0), 1, keepdims=True)
-        return (column == lane_ids).astype(F32)
+        lane = lax.broadcasted_iota(jnp.int32, (frames, 128), 1).astype(F32)
+        for r in range(small_rows):
+            block = (column - r * 128.0 == lane).astype(F32)
+            oh_v[:, r * 128:(r + 1) * 128] = block.astype(BF)
+            sm_c[0, pl.ds(level * small_rows + r, 1), :] = jnp.sum(block, 0, keepdims=True)
 
     per_q = book // zl_n
     per_c = nx * ny * rs
@@ -156,14 +161,6 @@
         ids = q * per_q + side * per_c + (xx * ny + yy) * rs + i
         return (ids.astype(F32) == code_rows[level:level + 1, :]).astype(F32).astype(BF)
 
-    small_rows = book // 128
-    oh0 = onehot(0)
-    oh1 = onehot(1)
-    for level, oh in enumerate((oh0, oh1)):
-        count = jnp.sum(oh, 0, keepdims=True)
-        for r in range(small_rows):
-            sm_c[0, pl.ds(level * small_rows + r, 1), :] = count[:, r * 128:(r + 1) * 128]
-
     @pl.when(zl == 0)
     def _():
         halo_v[...] = jnp.zeros(halo_v.shape, BF)
@@ -178,19 +175,20 @@
     spread(6, 0)
     spread(7, 1)
     loads[2].wait()
+    loads[6].wait()
     conv = acc_v[...] + dot(unf[:, :half], cw_v[:half, :])
     hid[...] = (conv + conv_b[...]).astype(BF)
     loads[3].wait()
     lat[...] = dot(hid[...], pw_v[...])
 
+    loads[5].wait()
+    code_rows = codes[0].astype(F32)
+
     def level_sums(level, ref0, refc):
-        value = lat[...]
-        hi = value.astype(BF)
-        lo = (value - hi.astype(F32)).astype(BF)
+        value = lat[...].astype(BF)
 
         def part(side):
-            oh = onehot_t(level, side)
-            made = dot(oh, hi) + dot(oh, lo)
+            made = dot(onehot_t(level, side), value)
             ref0[side] = made.astype(BF).reshape(ref0.shape[1:])
 
         part(1 - c)
@@ -199,9 +197,9 @@
         return copy
 
     s0_core = level_sums(0, s0_0, s0_c)
+    onehot(0)
     loads[4].wait()
-    r1 = lat[...] - dot(oh0.astype(BF), books_v[0])
-    lat[...] = r1
+    lat[...] = lat[...] - dot(oh_v[...], books_v[0])
     s1_core = level_sums(1, s1_0, s1_c)
 
     def stage1(core_copy, ref0, refc, ref1, refr, ring, n, me):
@@ -224,14 +222,14 @@
             made = made + refr2[d].astype(F32)
         return made
 
-    s0_x = stage1(s0_core, s0_0, s0_c, s0_1, s0_r1, at_x, nx, x)
-
+    onehot(1)
     value = lat[...]
-    lg = (value + (value - dot(oh1.astype(BF), books_v[1]))).astype(BF)
+    lg = (value + (value - dot(oh_v[...], books_v[1]))).astype(BF)
     lg_v[...] = lg
     pr_0[...] = dot(hid[...], lg, 0, 0).astype(BF).reshape(pr_0.shape)
     pr_core = sems.start(pr_0.at[1 - c], pr_c, at_core())
 
+    s0_x = stage1(s0_core, s0_0, s0_c, s0_1, s0_r1, at_x, nx, x)
     s1_y = stage1(s1_core, s1_0, s1_c, s1_1, s1_r1, at_y, ny, y)
 
     hg = dot(lg, pw_v[...], 1, 1).astype(BF)
@@ -253,21 +251,21 @@
     sm_core = sems.start(sm_c.at[0], sm_c.at[1], at_core())
 
     def corr(base, ref0, x_first):
-        group = nx * NC * tile
+        group = ny * nx * NC * tile
         for zz in range(zhh):
+            start = base + zz * group
+            made = dot(unf[:, start:start + group], lg_v[...], 0, 0).astype(BF)
             for yy in range(ny):
-                start = base + (zz * ny + yy) * group
-                made = dot(unf[:, start:start + group], lg_v[...], 0, 0).astype(BF)
                 for xx in range(nx):
                     for cc in range(NC):
-                        at = (xx * NC + cc) * tile
+                        at = ((yy * nx + xx) * NC + cc) * tile
                         a, b = (xx, yy) if x_first else (yy, xx)
                         row = (b * zhh + zz) * tile
                         ref0[cc, a, row:row + tile, :] = made[at:at + tile, :]
 
+    pr_x = stage1(pr_core, pr_0, pr_c, pr_1, pr_r1, at_x, nx, x)
     corr(0, ca_0, True)
     ca_core = sems.start(ca_0.at[1 - c], ca_c, at_core())
-    pr_x = stage1(pr_core, pr_0, pr_c, pr_1, pr_r1, at_x, nx, x)
     corr(half, cb_0, False)
     cb_core = sems.start(cb_0.at[1 - c], cb_c, at_core())
 
@@ -343,9 +341,7 @@
     cb_x = stage2(cb_y, cb_1, cb_r1, cb_2, cb_r2, at_x, nx, x, y)
 
     for k in range(lanes):
-        fg_v[:, k * 128:(k + 1) * 128] = fg_f[k].astype(BF)
-    fg_store = pltpu.make_async_copy(fg_v, fg_out, out_sem.at[0])
-    fg_store.start()
+        fg_out[:, k * 128:(k + 1) * 128] = fg_f[k].astype(BF)
 
     ca_d = finish(ca_y, ca_2, ca_r2, y)
     cb_d = finish(cb_x, cb_2, cb_r2, x)
@@ -363,73 +359,88 @@
     for level in range(2):
         row = sm_f[pl.ds(level * small_rows + zl * q_rows + base // 128, 1), :]
         columns.append(jnp.sum(jnp.where(ids == base % 128, row, 0.0), 1, keepdims=True))
+    counts = jnp.maximum(jnp.concatenate(columns, 0), 1.0)
+
+    done = summed(zh_c, zh_r, zh, zh_n)
+    ag_s[c, x, y] = (done[:2 * rs] / counts).astype(BF)
+    ag_p[c, y, x] = done[2 * rs:].astype(BF)
+    gs = [sems.start(ag_s.at[c, x, y], ag_s.at[c, x, y], at_y(d)) for d in range(1, ny)]
+    gp = [sems.start(ag_p.at[c, y, x], ag_p.at[c, y, x], at_x(d)) for d in range(1, nx)]
+
+    def gathered(sem_copies, ref_of, n, me):
+        for d, copy in enumerate(sem_copies):
+            src = (me - (d + 1) + n) % n
+            sems.arrived(copy, ref_of(src), at_core())
+
+    gathered(gs, lambda j: ag_s.at[c, x, j], ny, y)
+    gs2 = [sems.start(ag_s.at[c, x], ag_s.at[c, x], at_x(d)) for d in range(1, nx)]
+    gathered(gp, lambda j: ag_p.at[c, y, j], nx, x)
+    gp2 = [sems.start(ag_p.at[c, y], ag_p.at[c, y], at_y(d)) for d in range(1, ny)]
+    gs3 = [(x, sems.start(ag_s.at[c, x], ag_s.at[c, x], at_core()))]
+    gp3 = [(y, sems.start(ag_p.at[c, y], ag_p.at[c, y], at_core()))]
+
+    cl_r[0] = summed(ch_c, ch_r, zh, zh_n).astype(BF)
+    cl_c = [sems.start(cl_r.at[0], cl_r.at[d], at_l(d)) for d in range(1, zl_n)]
+
+    for d in range(1, max(nx, ny)):
+        if d < nx:
+            j = (x - d + nx) % nx
+            sems.arrived(gs2[d - 1], ag_s.at[c, j], at_core())
+            gs3.append((j, sems.start(ag_s.at[c, j], ag_s.at[c, j], at_core())))
+        if d < ny:
+            j = (y - d + ny) % ny
+            sems.arrived(gp2[d - 1], ag_p.at[c, j], at_core())
+            gp3.append((j, sems.start(ag_p.at[c, j], ag_p.at[c, j], at_core())))
+
+    owned = summed(cl_c, cl_r, zl, zl_n)
+    top = owned.astype(BF)
+    low = (owned - top.astype(F32)).astype(BF)
+    conv_f[...] = (dot(top, pw_v[...], 1, 1) + dot(low, pw_v[...], 1, 1)) / total
+    for j, copy in gs3:
+        sems.arrived(copy, ag_s.at[1 - c, j], at_core())
+    for j, copy in gp3:
+        sems.arrived(copy, ag_p.at[1 - c, j], at_core())
+
+    for copy in sems.started:
+        copy.wait_send()
+
+    @pl.when(zl < zl_n - 1)
+    def _():
+        halo.wait_send()
+
+    @pl.when(zl > 0)
+    def _():
+        nxt.wait_send()
+
+
+def assemble(g, fg_in, conv_f, sm_f, ag_s, ag_p, fg_out, conv_out, bias_out, proj_out, means_out, usage_out):
+    nx, ny, zl_n, book, total = g["nx"], g["ny"], g["zl"], g["book"], g["total"]
+    rs, rp, rpd, lanes = g["rs"], g["rp"], g["rpd"], g["chan"] // 128
+    zl = lax.axis_index("tm")
+    fg_out[...] = fg_in[...]
+    picked = None
+    for q in range(zl_n):
+        piece = jnp.where(zl == q, conv_f[q * rpd:(q + 1) * rpd, :], 0.0)
+        picked = piece if picked is None else picked + piece
+    conv_out[...] = picked
+    small_rows = book // 128
+    q_rows = small_rows // zl_n
+    per_c = nx * ny * rs
+    for level in range(2):
         for r in range(q_rows):
             count = sm_f[pl.ds(level * small_rows + zl * q_rows + r, 1), :]
             usage_out[level:level + 1, r * 128:(r + 1) * 128] = count * (book / total)
     for r in range(lanes):
         bias_out[:, r * 128:(r + 1) * 128] = sm_f[2 * small_rows + r:2 * small_rows + r + 1, :] / total
-    counts = jnp.maximum(jnp.concatenate(columns, 0), 1.0)
-
-    done = summed(zh_c, zh_r, zh, zh_n)
-    ag_s[c, x, y] = (done[:2 * rs] / counts).astype(BF)
-    ag_p[c, y, x] = done[2 * rs:].astype(BF)
-    gs = [sems.start(ag_s.at[c, x, y], ag_s.at[c, x, y], at_y(d)) for d in range(1, ny)]
-    gp = [sems.start(ag_p.at[c, y, x], ag_p.at[c, y, x], at_x(d)) for d in range(1, nx)]
-
-    def gathered(sem_copies, ref_of, n, me):
-        for d, copy in enumerate(sem_copies):
-            src = (me - (d + 1) + n) % n
-            sems.arrived(copy, ref_of(src), at_core())
-
-    gathered(gs, lambda j: ag_s.at[c, x, j], ny, y)
-    gs2 = [sems.start(ag_s.at[c, x], ag_s.at[c, x], at_x(d)) for d in range(1, nx)]
-    gathered(gp, lambda j: ag_p.at[c, y, j], nx, x)
-    gp2 = [sems.start(ag_p.at[c, y], ag_p.at[c, y], at_y(d)) for d in range(1, ny)]
-
-    cl_r[0] = summed(ch_c, ch_r, zh, zh_n).astype(BF)
-    cl_c = [sems.start(cl_r.at[0], cl_r.at[d], at_l(d)) for d in range(1, zl_n)]
-
-    gathered(gs2, lambda j: ag_s.at[c, j], nx, x)
-    gs3 = sems.start(ag_s.at[c], ag_s.at[c], at_core())
-    gathered(gp2, lambda j: ag_p.at[c, j], ny, y)
-    gp3 = sems.start(ag_p.at[c], ag_p.at[c], at_core())
-
-    owned = summed(cl_c, cl_r, zl, zl_n)
-    top = owned.astype(BF)
-    low = (owned - top.astype(F32)).astype(BF)
-    made = (dot(top, pw_v[...], 1, 1) + dot(low, pw_v[...], 1, 1)) / total
-    conv_f[...] = made
-    picked = None
-    for q in range(zl_n):
-        piece = jnp.where(zl == q, conv_f[q * rpd:(q + 1) * rpd, :], 0.0)
-        picked = piece if picked is None else picked + piece
-    conv_out[...] = picked
-
-    gathered([gs3], lambda j: ag_s.at[1 - c], 1, 0)
     for cc in range(NC):
         for xx in range(nx):
             for level in range(2):
                 rows = [ag_s[cc, xx, yy].astype(F32)[level * rs:(level + 1) * rs] for yy in range(ny)]
                 at = cc * per_c + xx * ny * rs
                 means_out[level, at:at + ny * rs, :] = jnp.concatenate(rows, 0).astype(BF)
-    gathered([gp3], lambda j: ag_p.at[1 - c], 1, 0)
-    for cc in range(NC):
-        for xx in range(nx):
             for yy in range(ny):
                 at = ((cc * nx + xx) * ny + yy) * rp
                 proj_out[at:at + rp, :] = ag_p[cc, yy, xx].astype(F32) * (1.0 / total)
-
-    fg_store.wait()
-    for copy in sems.started:
-        copy.wait_send()
-
-    @pl.when(zl < zl_n - 1)
-    def _():
-        halo.wait_send()
-
-    @pl.when(zl > 0)
-    def _():
-        nxt.wait_send()
 
 
 def shards(g, feats, codes, conv_weight, conv_bias, proj_weight, codebooks):
@@ -460,9 +471,12 @@
     zrows = 2 * rs + rp
     scratch = [
         pltpu.VMEM((rows_in, chan), BF),
+        pltpu.VMEM((1, 2, frames), jnp.int32),
         pltpu.VMEM((taps, chan), BF),
+        pltpu.VMEM((1, chan), F32),
         pltpu.VMEM((chan, dz), BF),
         pltpu.VMEM((2, book, dz), BF),
+        pltpu.VMEM((frames, book), BF),
         pltpu.VMEM((lanes, rows_in + 8, 128), F32),
         pltpu.VMEM((frames, taps), BF),
         pltpu.VMEM((frames, chan), F32),
@@ -473,7 +487,6 @@
         pltpu.VMEM((16, chan), BF),
         pltpu.VMEM((16, chan), BF),
         pltpu.VMEM((lanes, rows_in, 128), F32),
-        pltpu.VMEM((rows_in, chan), BF),
     ]
     scratch += flow(nx, ny, zln * rs)
     scratch += flow(ny, nx, zln * rs)
@@ -482,25 +495,36 @@
     scratch += flow(ny, nx, zhn // 2 * tile)
     scratch += [pltpu.VMEM((n, small, 128), F32) for n in (NC, nx, ny, zln, zhn)]
     scratch += [
-        pltpu.VMEM((small, 128), F32),
         pltpu.VMEM((zln, zrows, dz), BF),
         pltpu.VMEM((zln, zrows, dz), BF),
         pltpu.VMEM((zhn, zrows, dz), BF),
         pltpu.VMEM((zhn, tile, dz), BF),
         pltpu.VMEM((zhn, tile, dz), BF),
         pltpu.VMEM((zln, tile, dz), BF),
-        pltpu.VMEM((tile, chan), F32),
-        pltpu.VMEM((NC, nx, ny, 2 * rs, dz), BF),
-        pltpu.VMEM((NC, ny, nx, rp, dz), BF),
-        pltpu.SemaphoreType.DMA((5,)),
-        pltpu.SemaphoreType.DMA((1,)),
+        pltpu.SemaphoreType.DMA((7,)),
         pltpu.SemaphoreType.DMA((96,)),
         pltpu.SemaphoreType.DMA((96,)),
     ]
-    any_spec = pl.BlockSpec(memory_space=pl.ANY)
+    hbm = pl.BlockSpec(memory_space=pltpu.HBM)
     vmem = pl.BlockSpec(memory_space=pltpu.VMEM)
-    out = pl.pallas_call(
+    fg, conv_f, sm_f, ag_s, ag_p = pl.pallas_call(
         functools.partial(kernel, g),
+        out_shape=(
+            pltpu.VMEM((rows_in, chan), BF),
+            pltpu.VMEM((tile, chan), F32),
+            pltpu.VMEM((small, 128), F32),
+            pltpu.VMEM((NC, nx, ny, 2 * rs, dz), BF),
+            pltpu.VMEM((NC, ny, nx, rp, dz), BF),
+        ),
+        in_specs=[hbm] * 6,
+        out_specs=(vmem,) * 5,
+        scratch_shapes=scratch,
+        compiler_params=pltpu.CompilerParams(
+            collective_id=0, has_side_effects=True, vmem_limit_bytes=32 << 20),
+    )(*[pltpu.with_memory_space_constraint(v, pltpu.HBM) for v in (
+        feats, codes, conv_weight, conv_bias.reshape(1, chan), proj_weight, codebooks)])
+    fg, cg, bg, pg, cm, cu = pl.pallas_call(
+        functools.partial(assemble, g),
         out_shape=(
             jax.ShapeDtypeStruct((rows_in, chan), BF),
             jax.ShapeDtypeStruct((rpd, chan), F32),
@@ -509,13 +533,10 @@
             jax.ShapeDtypeStruct((2, book // zln, dz), BF),
             jax.ShapeDtypeStruct((2, book // zln), F32),
         ),
-        in_specs=[any_spec, vmem, any_spec, vmem, any_spec, any_spec],
-        out_specs=(any_spec, vmem, vmem, vmem, vmem, vmem),
-        scratch_shapes=scratch,
-        compiler_params=pltpu.CompilerParams(
-            collective_id=0, has_side_effects=True, vmem_limit_bytes=56 << 20),
-    )(feats, codes, conv_weight, conv_bias.reshape(1, chan), proj_weight, codebooks)
-    fg, cg, bg, pg, cm, cu = out
+        in_specs=[vmem, vmem, vmem, vmem, vmem],
+        out_specs=(vmem, vmem, vmem, vmem, vmem, vmem),
+        compiler_params=pltpu.CompilerParams(vmem_limit_bytes=8 << 20),
+    )(fg, conv_f, sm_f, ag_s, ag_p)
     return fg, cg, bg.reshape(chan), pg, cm, cu
 
 

time: 68.1 us -> 59.3 us (0.87)
  local copies, waits for them, and re-layouts: 7.81 us -> 0 us
  Pallas kernels: 59.4 us -> 58.6 us
    unnamed x10 -> x0, local copies, waits for them, and re-layouts: 7.81 us -> none
    pallas_call x1 -> x2, Pallas kernels: 59.4 us -> 58.6 us  [the longest x1 57.3 us: shards(): pl.pallas_call(functools.partial(kernel, g), out_shape=(pltpu.VMEM((rows_...]
where the time goes in v2:
time: 59.3 us; the launch traced here: 59.2 us
  Pallas kernels  58.6 us (99%)
  between operations  0.64 us (1%)
    pallas_call x1, Pallas kernels, shards(): pl.pallas_call(functools.partial(kernel, g), out_shape=(pltpu.VMEM((rows_...  57.3 us
    pallas_call x1, Pallas kernels, shards(): pl.pallas_call(functools.partial(assemble, g), out_shape=(jax.ShapeDtypeS...  1.26 us

profile of v2, /device:TPU:1, one launch (start us, length us, event | category | flops | bytes accessed | tf_op | source)
XLA Modules:
  0.0 59.2 jit_solution(18171570068054682103)
XLA Ops:
  0.6 57.3 %shard_map.109 = (bf16[768,512]{1,0:T(8,128)(2,1)S(1)}, f32[16,512]{1,0:T(8,128)S(1)}, f32[24,128]{1,0:T(8,128)S(1)}, bf16[2,4,4,16,256]{4,3,2,1,0:T(8,128)(2,1)S(1)}, bf16[2,4,4,16,256]{4,3,2,1,0:T(8,128)(2,1)S(1)}) custom-call(bf16[768,512]{1,0:T(8,128)(2,1)} %feats.1, s32[1,2,384]{2,1,0:T(2,128)} %codes_in.1, bf16[2048,512]{1,0:T(8,128)(2,1)} %conv_w.1, ...), custom_call_target="tpu_custom_call" | custom-call | tf_op jit(solution)/shard_map/pallas_call | solution.py:510
  57.9 1.3 %shard_map.110 = (bf16[768,512]{1,0:T(8,128)(2,1)}, f32[4,512]{1,0:T(4,128)}, f32[1,512]{1,0:T(1,128)}, f32[512,256]{1,0:T(8,128)}, bf16[2,256,256]{2,1,0:T(8,128)(2,1)}, /*index=5*/f32[2,256]{1,0:T(2,128)}) custom-call(bf16[768,512]{1,0:T(8,128)(2,1)S(1)} %get-tuple-element.17.fg_in, f32[16,512]{1,0:T(8,128)S(1)} %get-tuple-element.18.conv_f, ...), custom_call_target="tpu_custom_call" | custom-call | tf_op jit(solution)/shard_map/pallas_call | solution.py:526

commit v3 on v2

--- a/solution.py
+++ b/solution.py
@@ -47,15 +47,15 @@
 
 def kernel(g, feats, codes_in, conv_w, conv_b_in, proj_w, books,
            fg_out, conv_f, sm_f, ag_s, ag_p,
-           feats_v, codes, cw_v, conv_b, pw_v, books_v, oh_v, fx, unf, acc_v, hid, lat, lg_v, hgf, halo_v, next_v, fg_f,
+           feats_v, codes, cw_v, conv_b, pw_v, books_v, oh_v, oht_v, fx, unf, acc_v, hid, lat, lg_v, hgf, halo_v, next_v, fg_f,
            s0_0, s0_c, s0_1, s0_r1, s0_2, s0_r2,
            s1_0, s1_c, s1_1, s1_r1, s1_2, s1_r2,
            pr_0, pr_c, pr_1, pr_r1, pr_2, pr_r2,
            ca_0, ca_c, ca_1, ca_r1, ca_2, ca_r2,
            cb_0, cb_c, cb_1, cb_r1, cb_2, cb_r2,
-           sm_c, sm_x, sm_y, sm_l, sm_h,
+           sm_c, sm_x, sm_y, sm_t, sm_q, sm_l, sm_h,
            zl_s, zl_r, zh_r, ch_s, ch_r, cl_r,
-           in_sem, send_sem, recv_sem):
+           in_sem, word_sem, send_sem, recv_sem):
     nx, ny, zh_n, zl_n = g["nx"], g["ny"], g["zh"], g["zl"]
     frames, chan, dz, book = g["frames"], g["chan"], g["dz"], g["book"]
     total = g["total"]
@@ -89,13 +89,6 @@
         return dev(c, x, y, (zh + d) % zh_n, zl)
 
     sems = Sems(send_sem, recv_sem)
-
-    barrier = pltpu.get_barrier_semaphore()
-    partners = [at_core()]
-    for ring, n in ((at_x, nx), (at_y, ny), (at_l, zl_n), (at_h, zh_n)):
-        partners += [ring(d) for d in range(1, n)]
-    for partner in partners:
-        pl.semaphore_signal(barrier, inc=1, device_id=partner, device_id_type=MESH)
 
     half = 2 * chan
     loads = [
@@ -110,6 +103,23 @@
     for load in loads:
         load.start()
 
+    ring_z = zh_n * zl_n
+    z = zh * zl_n + zl
+
+    def at_z(d):
+        zz = (z + d + ring_z) % ring_z
+        return dev(c, x, y, zz // zl_n, zz % zl_n)
+
+    reaches = [1]
+    while 2 * reaches[-1] < ring_z // 2:
+        reaches.append(2 * reaches[-1])
+    barrier = pltpu.get_barrier_semaphore()
+    partners = [at_core(), at_z(1), at_z(-1)]
+    for ring, n in ((at_x, nx), (at_y, ny), (at_l, zl_n)):
+        partners += [ring(d) for d in range(1, n)]
+    for partner in partners:
+        pl.semaphore_signal(barrier, inc=1, device_id=partner, device_id_type=MESH)
+
     rows_in = 2 * frames
     loads[0].wait()
     for k in range(lanes):
@@ -122,15 +132,9 @@
 
     spread(8, 2)
     spread(9, 3)
+    loads[5].wait()
     loads[1].wait()
-    acc_v[...] = dot(unf[:, half:], cw_v[half:, :])
-
-    pl.semaphore_wait(barrier, len(partners))
-    halo = sems.copy(feats_v.at[pl.ds(rows_in - 16, 16)], halo_v, at_l(1))
-
-    @pl.when(zl < zl_n - 1)
-    def _():
-        halo.start()
+    code_rows = codes[0].astype(F32)
 
     small_rows = book // 128
 
@@ -141,7 +145,7 @@
         lane = lax.broadcasted_iota(jnp.int32, (frames, 128), 1).astype(F32)
         for r in range(small_rows):
             block = (column - r * 128.0 == lane).astype(F32)
-            oh_v[:, r * 128:(r + 1) * 128] = block.astype(BF)
+            oh_v[level, :, r * 128:(r + 1) * 128] = block.astype(BF)
             sm_c[0, pl.ds(level * small_rows + r, 1), :] = jnp.sum(block, 0, keepdims=True)
 
     per_q = book // zl_n
@@ -161,6 +165,30 @@
         ids = q * per_q + side * per_c + (xx * ny + yy) * rs + i
         return (ids.astype(F32) == code_rows[level:level + 1, :]).astype(F32).astype(BF)
 
+    acc_v[...] = dot(unf[:, half:], cw_v[half:, :])
+    for level in range(2):
+        onehot(level)
+        for side in range(NC):
+            oht_v[level, side] = onehot_t(level, side)
+
+    pl.semaphore_wait(barrier, len(partners))
+
+    def tell(k):
+        if k < len(reaches):
+            for d in (reaches[k], -reaches[k]):
+                pl.semaphore_signal(word_sem.at[k], inc=1, device_id=at_z(d), device_id_type=MESH)
+
+    def told(k):
+        if k < len(reaches):
+            pl.semaphore_wait(word_sem.at[k], 2)
+
+    tell(0)
+    halo = sems.copy(feats_v.at[pl.ds(rows_in - 16, 16)], halo_v, at_l(1))
+
+    @pl.when(zl < zl_n - 1)
+    def _():
+        halo.start()
+
     @pl.when(zl == 0)
     def _():
         halo_v[...] = jnp.zeros(halo_v.shape, BF)
@@ -178,29 +206,22 @@
     loads[6].wait()
     conv = acc_v[...] + dot(unf[:, :half], cw_v[:half, :])
     hid[...] = (conv + conv_b[...]).astype(BF)
+    told(0)
+    tell(1)
     loads[3].wait()
     lat[...] = dot(hid[...], pw_v[...])
 
-    loads[5].wait()
-    code_rows = codes[0].astype(F32)
-
     def level_sums(level, ref0, refc):
         value = lat[...].astype(BF)
 
         def part(side):
-            made = dot(onehot_t(level, side), value)
+            made = dot(oht_v[level, side], value)
             ref0[side] = made.astype(BF).reshape(ref0.shape[1:])
 
         part(1 - c)
         copy = sems.start(ref0.at[1 - c], refc, at_core())
         part(c)
         return copy
-
-    s0_core = level_sums(0, s0_0, s0_c)
-    onehot(0)
-    loads[4].wait()
-    lat[...] = lat[...] - dot(oh_v[...], books_v[0])
-    s1_core = level_sums(1, s1_0, s1_c)
 
     def stage1(core_copy, ref0, refc, ref1, refr, ring, n, me):
         core_copy.wait_recv()
@@ -222,14 +243,20 @@
             made = made + refr2[d].astype(F32)
         return made
 
-    onehot(1)
+    s0_core = level_sums(0, s0_0, s0_c)
+    loads[4].wait()
+    lat[...] = lat[...] - dot(oh_v[0], books_v[0])
+    s1_core = level_sums(1, s1_0, s1_c)
+
+    s0_x = stage1(s0_core, s0_0, s0_c, s0_1, s0_r1, at_x, nx, x)
+
     value = lat[...]
-    lg = (value + (value - dot(oh_v[...], books_v[1]))).astype(BF)
+    lg = (value + (value - dot(oh_v[1], books_v[1]))).astype(BF)
     lg_v[...] = lg
     pr_0[...] = dot(hid[...], lg, 0, 0).astype(BF).reshape(pr_0.shape)
     pr_core = sems.start(pr_0.at[1 - c], pr_c, at_core())
-
-    s0_x = stage1(s0_core, s0_0, s0_c, s0_1, s0_r1, at_x, nx, x)
+    told(1)
+    tell(2)
     s1_y = stage1(s1_core, s1_0, s1_c, s1_1, s1_r1, at_y, ny, y)
 
     hg = dot(lg, pw_v[...], 1, 1).astype(BF)
@@ -263,9 +290,9 @@
                         row = (b * zhh + zz) * tile
                         ref0[cc, a, row:row + tile, :] = made[at:at + tile, :]
 
-    pr_x = stage1(pr_core, pr_0, pr_c, pr_1, pr_r1, at_x, nx, x)
     corr(0, ca_0, True)
     ca_core = sems.start(ca_0.at[1 - c], ca_c, at_core())
+    pr_x = stage1(pr_core, pr_0, pr_c, pr_1, pr_r1, at_x, nx, x)
     corr(half, cb_0, False)
     cb_core = sems.start(cb_0.at[1 - c], cb_c, at_core())
 
@@ -292,6 +319,25 @@
     ca_x = stage1(ca_core, ca_0, ca_c, ca_1, ca_r1, at_x, nx, x)
     cb_y = stage1(cb_core, cb_0, cb_c, cb_1, cb_r1, at_y, ny, y)
 
+    @pl.when(zl == zl_n - 1)
+    def _():
+        next_v[...] = jnp.zeros(next_v.shape, BF)
+
+    @pl.when(zl < zl_n - 1)
+    def _():
+        nxt.wait_recv()
+
+    hgf[pl.ds(frames, 8), :] = next_v[...].astype(F32)[0:8, :]
+    lg_next = hgf[pl.ds(1, frames), :].astype(BF)
+
+    def feat_part(part):
+        made = (dot(lg_next, cw_v[pl.ds(part * chan, chan), :], 1, 1)
+                + dot(hid[...], cw_v[pl.ds(half + part * chan, chan), :], 1, 1))
+        for k in range(lanes):
+            fg_f[k, pl.ds(part, frames, stride=2), :] = made[:, k * 128:(k + 1) * 128]
+
+    feat_part(0)
+
     s0_d = finish(s0_y, s0_2, s0_r2, y)
     s1_d = finish(s1_x, s1_2, s1_r2, x)
     pr_d = finish(pr_y, pr_2, pr_r2, y)
@@ -300,28 +346,18 @@
             [s0_d[q * rs:(q + 1) * rs], s1_d[q * rs:(q + 1) * rs], pr_d], 0).astype(BF)
     zl_c = [sems.start(zl_s.at[(zl + d) % zl_n], zl_r.at[d], at_l(d)) for d in range(1, zl_n)]
     zl_r[0] = zl_s[zl]
-    small(sm_ys, sm_y, y, ny, sm_l.at[0])
-    sm_ls = small_send(sm_l, at_l, zl_n)
-
-    @pl.when(zl == zl_n - 1)
-    def _():
-        next_v[...] = jnp.zeros(next_v.shape, BF)
-
-    @pl.when(zl < zl_n - 1)
-    def _():
-        nxt.wait_recv()
-
-    hgf[pl.ds(frames, 8), :] = next_v[...].astype(F32)[0:8, :]
-    lg_next = hgf[pl.ds(1, frames), :].astype(BF)
-
-    def feat_part(part):
-        made = (dot(lg_next, cw_v[pl.ds(part * chan, chan), :], 1, 1)
-                + dot(hid[...], cw_v[pl.ds(half + part * chan, chan), :], 1, 1))
-        for k in range(lanes):
-            fg_f[k, pl.ds(part, frames, stride=2), :] = made[:, k * 128:(k + 1) * 128]
-
-    feat_part(0)
-    feat_part(1)
+    small(sm_ys, sm_y, y, ny, sm_t)
+    q_rows = per_q // 128
+    for q in range(zl_n):
+        for level in range(2):
+            at = level * small_rows + q * q_rows
+            sm_q[q, level * q_rows:(level + 1) * q_rows, :] = sm_t[at:at + q_rows, :]
+        sm_q[q, 2 * q_rows:2 * q_rows + lanes, :] = sm_t[2 * small_rows:2 * small_rows + lanes, :]
+        rest = sm_q.shape[1] - 2 * q_rows - lanes
+        if rest:
+            sm_q[q, 2 * q_rows + lanes:, :] = jnp.zeros((rest, 128), F32)
+    sm_ls = [sems.start(sm_q.at[(zl + d) % zl_n], sm_l.at[d], at_l(d)) for d in range(1, zl_n)]
+    sm_l[0] = sm_q[zl]
 
     def summed(copies, ref, me, n):
         for copy in copies:
@@ -332,16 +368,14 @@
             made = piece if made is None else made + piece
         return made
 
+    ca_y = stage2(ca_x, ca_1, ca_r1, ca_2, ca_r2, at_y, ny, y, x)
+    cb_x = stage2(cb_y, cb_1, cb_r1, cb_2, cb_r2, at_x, nx, x, y)
+
+    told(2)
     zh_r[0] = summed(zl_c, zl_r, zl, zl_n).astype(BF)
     zh_c = [sems.start(zh_r.at[0], zh_r.at[d], at_h(d)) for d in range(1, zh_n)]
     small(sm_ls, sm_l, zl, zl_n, sm_h.at[0])
     sm_hs = small_send(sm_h, at_h, zh_n)
-
-    ca_y = stage2(ca_x, ca_1, ca_r1, ca_2, ca_r2, at_y, ny, y, x)
-    cb_x = stage2(cb_y, cb_1, cb_r1, cb_2, cb_r2, at_x, nx, x, y)
-
-    for k in range(lanes):
-        fg_out[:, k * 128:(k + 1) * 128] = fg_f[k].astype(BF)
 
     ca_d = finish(ca_y, ca_2, ca_r2, y)
     cb_d = finish(cb_x, cb_2, cb_r2, x)
@@ -351,13 +385,16 @@
     ch_c = [sems.start(ch_s.at[(zh + d) % zh_n], ch_r.at[d], at_h(d)) for d in range(1, zh_n)]
     ch_r[0] = ch_s[zh]
 
+    feat_part(1)
+    for k in range(lanes):
+        fg_out[:, k * 128:(k + 1) * 128] = fg_f[k].astype(BF)
+
     small(sm_hs, sm_h, zh, zh_n, sm_f)
-    q_rows = per_q // 128
     base = c * per_c + (x * ny + y) * rs
     ids = lax.broadcasted_iota(jnp.int32, (rs, 128), 1) - lax.broadcasted_iota(jnp.int32, (rs, 128), 0)
     columns = []
     for level in range(2):
-        row = sm_f[pl.ds(level * small_rows + zl * q_rows + base // 128, 1), :]
+        row = sm_f[pl.ds(level * q_rows + base // 128, 1), :]
         columns.append(jnp.sum(jnp.where(ids == base % 128, row, 0.0), 1, keepdims=True))
     counts = jnp.maximum(jnp.concatenate(columns, 0), 1.0)
 
@@ -428,10 +465,10 @@
     per_c = nx * ny * rs
     for level in range(2):
         for r in range(q_rows):
-            count = sm_f[pl.ds(level * small_rows + zl * q_rows + r, 1), :]
+            count = sm_f[level * q_rows + r:level * q_rows + r + 1, :]
             usage_out[level:level + 1, r * 128:(r + 1) * 128] = count * (book / total)
     for r in range(lanes):
-        bias_out[:, r * 128:(r + 1) * 128] = sm_f[2 * small_rows + r:2 * small_rows + r + 1, :] / total
+        bias_out[:, r * 128:(r + 1) * 128] = sm_f[2 * q_rows + r:2 * q_rows + r + 1, :] / total
     for cc in range(NC):
         for xx in range(nx):
             for level in range(2):
@@ -468,6 +505,7 @@
         ]
 
     small = -(-(2 * book // 128 + lanes) // 8) * 8
+    few = -(-(2 * book // zln // 128 + lanes) // 8) * 8
     zrows = 2 * rs + rp
     scratch = [
         pltpu.VMEM((rows_in, chan), BF),
@@ -476,7 +514,8 @@
         pltpu.VMEM((1, chan), F32),
         pltpu.VMEM((chan, dz), BF),
         pltpu.VMEM((2, book, dz), BF),
-        pltpu.VMEM((frames, book), BF),
+        pltpu.VMEM((2, frames, book), BF),
+        pltpu.VMEM((2, NC, book // NC, frames), BF),
         pltpu.VMEM((lanes, rows_in + 8, 128), F32),
         pltpu.VMEM((frames, taps), BF),
         pltpu.VMEM((frames, chan), F32),
@@ -493,7 +532,8 @@
     scratch += flow(nx, ny, rp)
     scratch += flow(nx, ny, zhn // 2 * tile)
     scratch += flow(ny, nx, zhn // 2 * tile)
-    scratch += [pltpu.VMEM((n, small, 128), F32) for n in (NC, nx, ny, zln, zhn)]
+    scratch += [pltpu.VMEM((n, small, 128), F32) for n in (NC, nx, ny)] + [pltpu.VMEM((small, 128), F32)]
+    scratch += [pltpu.VMEM((n, few, 128), F32) for n in (zln, zln, zhn)]
     scratch += [
         pltpu.VMEM((zln, zrows, dz), BF),
         pltpu.VMEM((zln, zrows, dz), BF),
@@ -502,6 +542,7 @@
         pltpu.VMEM((zhn, tile, dz), BF),
         pltpu.VMEM((zln, tile, dz), BF),
         pltpu.SemaphoreType.DMA((7,)),
+        pltpu.SemaphoreType.REGULAR((3,)),
         pltpu.SemaphoreType.DMA((96,)),
         pltpu.SemaphoreType.DMA((96,)),
     ]
@@ -512,7 +553,7 @@
         out_shape=(
             pltpu.VMEM((rows_in, chan), BF),
             pltpu.VMEM((tile, chan), F32),
-            pltpu.VMEM((small, 128), F32),
+            pltpu.VMEM((few, 128), F32),
             pltpu.VMEM((NC, nx, ny, 2 * rs, dz), BF),
             pltpu.VMEM((NC, ny, nx, rp, dz), BF),
         ),

time: 59.3 us -> 57.4 us (0.968)
  Pallas kernels: 58.6 us -> 56.6 us
    pallas_call x1, Pallas kernels: 57.3 us -> 55.4 us  [shards(): pl.pallas_call(functools.partial(kernel, g), out_shape=(pltpu.VMEM((rows_...]
where the time goes in v3:
time: 57.4 us; the launch traced here: 57.3 us
  Pallas kernels  56.6 us (99%)
  between operations  0.64 us (1%)
    pallas_call x1, Pallas kernels, shards(): pl.pallas_call(functools.partial(kernel, g), out_shape=(pltpu.VMEM((rows_...  55.4 us
    pallas_call x1, Pallas kernels, shards(): pl.pallas_call(functools.partial(assemble, g), out_shape=(jax.ShapeDtypeS...  1.26 us

profile of v3, /device:TPU:1, one launch (start us, length us, event | category | flops | bytes accessed | tf_op | source)
XLA Modules:
  0.0 57.3 jit_solution(9022548999009125591)
XLA Ops:
  0.6 55.4 %shard_map.109 = (bf16[768,512]{1,0:T(8,128)(2,1)S(1)}, f32[16,512]{1,0:T(8,128)S(1)}, f32[8,128]{1,0:T(8,128)S(1)}, bf16[2,4,4,16,256]{4,3,2,1,0:T(8,128)(2,1)S(1)}, bf16[2,4,4,16,256]{4,3,2,1,0:T(8,128)(2,1)S(1)}) custom-call(bf16[768,512]{1,0:T(8,128)(2,1)} %feats.1, s32[1,2,384]{2,1,0:T(2,128)} %codes_in.1, bf16[2048,512]{1,0:T(8,128)(2,1)} %conv_w.1, ...), custom_call_target="tpu_custom_call" | custom-call | tf_op jit(solution)/shard_map/pallas_call | solution.py:551
  56.0 1.3 %shard_map.110 = (bf16[768,512]{1,0:T(8,128)(2,1)}, f32[4,512]{1,0:T(4,128)}, f32[1,512]{1,0:T(1,128)}, f32[512,256]{1,0:T(8,128)}, bf16[2,256,256]{2,1,0:T(8,128)(2,1)}, /*index=5*/f32[2,256]{1,0:T(2,128)}) custom-call(bf16[768,512]{1,0:T(8,128)(2,1)S(1)} %get-tuple-element.17.fg_in, f32[16,512]{1,0:T(8,128)S(1)} %get-tuple-element.18.conv_f, ...), custom_call_target="tpu_custom_call" | custom-call | tf_op jit(solution)/shard_map/pallas_call | solution.py:567

commit v4 on v3

--- a/solution.py
+++ b/solution.py
@@ -11,6 +11,10 @@
 BF = jnp.bfloat16
 F32 = jnp.float32
 NC = 2
+
+
+def far_first(n):
+    return sorted(range(1, n), key=lambda d: -min(d, n - d))
 
 
 def dot(a, b, ca=1, cb=0):
@@ -31,6 +35,10 @@
         self.index[id(made)] = index
         return made
 
+    def ring(self, n, src, dst, device):
+        made = {d: self.start(src(d), dst(d), device(d)) for d in far_first(n)}
+        return [made[d] for d in range(1, n)]
+
     def arrived(self, made, ref, device):
         index = self.index[id(made)]
         pltpu.make_async_remote_copy(
@@ -46,7 +54,7 @@
 
 
 def kernel(g, feats, codes_in, conv_w, conv_b_in, proj_w, books,
-           fg_out, conv_f, sm_f, ag_s, ag_p,
+           fg_out, conv_f, sm_f, ag,
            feats_v, codes, cw_v, conv_b, pw_v, books_v, oh_v, oht_v, fx, unf, acc_v, hid, lat, lg_v, hgf, halo_v, next_v, fg_f,
            s0_0, s0_c, s0_1, s0_r1, s0_2, s0_r2,
            s1_0, s1_c, s1_1, s1_r1, s1_2, s1_r2,
@@ -226,7 +234,7 @@
     def stage1(core_copy, ref0, refc, ref1, refr, ring, n, me):
         core_copy.wait_recv()
         ref1[...] = (ref0[c].astype(F32) + refc[...].astype(F32)).astype(BF)
-        return [sems.start(ref1.at[(me + d) % n], refr.at[d - 1], ring(d)) for d in range(1, n)]
+        return sems.ring(n, lambda d: ref1.at[(me + d) % n], lambda d: refr.at[d - 1], ring)
 
     def stage2(copies, ref1, refr, ref2, refr2, ring, n, me, me1):
         made = ref1[me1].astype(F32)
@@ -234,7 +242,7 @@
             copy.wait_recv()
             made = made + refr[d].astype(F32)
         ref2[...] = made.astype(BF).reshape(ref2.shape)
-        return [sems.start(ref2.at[(me + d) % n], refr2.at[d - 1], ring(d)) for d in range(1, n)]
+        return sems.ring(n, lambda d: ref2.at[(me + d) % n], lambda d: refr2.at[d - 1], ring)
 
     def finish(copies, ref2, refr2, me):
         made = ref2[me].astype(F32)
@@ -306,7 +314,7 @@
         nxt_ref[...] = made
 
     def small_send(ref, ring, n):
-        return [sems.start(ref.at[0], ref.at[d], ring(d)) for d in range(1, n)]
+        return sems.ring(n, lambda d: ref.at[0], lambda d: ref.at[d], ring)
 
     small([sm_core], sm_c, c, NC, sm_x.at[0])
     sm_xs = small_send(sm_x, at_x, nx)
@@ -344,7 +352,7 @@
     for q in range(zl_n):
         zl_s[q] = jnp.concatenate(
             [s0_d[q * rs:(q + 1) * rs], s1_d[q * rs:(q + 1) * rs], pr_d], 0).astype(BF)
-    zl_c = [sems.start(zl_s.at[(zl + d) % zl_n], zl_r.at[d], at_l(d)) for d in range(1, zl_n)]
+    zl_c = sems.ring(zl_n, lambda d: zl_s.at[(zl + d) % zl_n], lambda d: zl_r.at[d], at_l)
     zl_r[0] = zl_s[zl]
     small(sm_ys, sm_y, y, ny, sm_t)
     q_rows = per_q // 128
@@ -373,7 +381,7 @@
 
     told(2)
     zh_r[0] = summed(zl_c, zl_r, zl, zl_n).astype(BF)
-    zh_c = [sems.start(zh_r.at[0], zh_r.at[d], at_h(d)) for d in range(1, zh_n)]
+    zh_c = sems.ring(zh_n, lambda d: zh_r.at[0], lambda d: zh_r.at[d], at_h)
     small(sm_ls, sm_l, zl, zl_n, sm_h.at[0])
     sm_hs = small_send(sm_h, at_h, zh_n)
 
@@ -382,7 +390,7 @@
     for zz in range(zhh):
         ch_s[zz] = ca_d[zz * tile:(zz + 1) * tile].astype(BF)
         ch_s[zhh + zz] = cb_d[zz * tile:(zz + 1) * tile].astype(BF)
-    ch_c = [sems.start(ch_s.at[(zh + d) % zh_n], ch_r.at[d], at_h(d)) for d in range(1, zh_n)]
+    ch_c = sems.ring(zh_n, lambda d: ch_s.at[(zh + d) % zh_n], lambda d: ch_r.at[d], at_h)
     ch_r[0] = ch_s[zh]
 
     feat_part(1)
@@ -399,44 +407,32 @@
     counts = jnp.maximum(jnp.concatenate(columns, 0), 1.0)
 
     done = summed(zh_c, zh_r, zh, zh_n)
-    ag_s[c, x, y] = (done[:2 * rs] / counts).astype(BF)
-    ag_p[c, y, x] = done[2 * rs:].astype(BF)
-    gs = [sems.start(ag_s.at[c, x, y], ag_s.at[c, x, y], at_y(d)) for d in range(1, ny)]
-    gp = [sems.start(ag_p.at[c, y, x], ag_p.at[c, y, x], at_x(d)) for d in range(1, nx)]
-
-    def gathered(sem_copies, ref_of, n, me):
-        for d, copy in enumerate(sem_copies):
-            src = (me - (d + 1) + n) % n
-            sems.arrived(copy, ref_of(src), at_core())
-
-    gathered(gs, lambda j: ag_s.at[c, x, j], ny, y)
-    gs2 = [sems.start(ag_s.at[c, x], ag_s.at[c, x], at_x(d)) for d in range(1, nx)]
-    gathered(gp, lambda j: ag_p.at[c, y, j], nx, x)
-    gp2 = [sems.start(ag_p.at[c, y], ag_p.at[c, y], at_y(d)) for d in range(1, ny)]
-    gs3 = [(x, sems.start(ag_s.at[c, x], ag_s.at[c, x], at_core()))]
-    gp3 = [(y, sems.start(ag_p.at[c, y], ag_p.at[c, y], at_core()))]
+    ag[c, x, y] = jnp.concatenate([done[:2 * rs] / counts, done[2 * rs:]], 0).astype(BF)
+    steps = [(dx, dy) for dx in range(nx) for dy in range(ny) if dx or dy]
+    steps.sort(key=lambda s: -(min(s[0], nx - s[0]) + min(s[1], ny - s[1])))
+    plane = {
+        (dx, dy): sems.start(ag.at[c, x, y], ag.at[c, x, y], dev(c, (x + dx) % nx, (y + dy) % ny, zh, zl))
+        for dx, dy in steps
+    }
 
     cl_r[0] = summed(ch_c, ch_r, zh, zh_n).astype(BF)
     cl_c = [sems.start(cl_r.at[0], cl_r.at[d], at_l(d)) for d in range(1, zl_n)]
 
-    for d in range(1, max(nx, ny)):
-        if d < nx:
-            j = (x - d + nx) % nx
-            sems.arrived(gs2[d - 1], ag_s.at[c, j], at_core())
-            gs3.append((j, sems.start(ag_s.at[c, j], ag_s.at[c, j], at_core())))
-        if d < ny:
-            j = (y - d + ny) % ny
-            sems.arrived(gp2[d - 1], ag_p.at[c, j], at_core())
-            gp3.append((j, sems.start(ag_p.at[c, j], ag_p.at[c, j], at_core())))
+    rows_in_order = sorted(range(nx), key=lambda d: min(d, nx - d))
+    others = []
+    for dx in rows_in_order:
+        j = (x - dx + nx) % nx
+        for dy in range(ny):
+            if dx or dy:
+                sems.arrived(plane[dx, dy], ag.at[c, j, (y - dy + ny) % ny], at_core())
+        others.append((j, sems.start(ag.at[c, j], ag.at[c, j], at_core())))
 
     owned = summed(cl_c, cl_r, zl, zl_n)
     top = owned.astype(BF)
     low = (owned - top.astype(F32)).astype(BF)
     conv_f[...] = (dot(top, pw_v[...], 1, 1) + dot(low, pw_v[...], 1, 1)) / total
-    for j, copy in gs3:
-        sems.arrived(copy, ag_s.at[1 - c, j], at_core())
-    for j, copy in gp3:
-        sems.arrived(copy, ag_p.at[1 - c, j], at_core())
+    for j, copy in others:
+        sems.arrived(copy, ag.at[1 - c, j], at_core())
 
     for copy in sems.started:
         copy.wait_send()
@@ -450,7 +446,7 @@
         nxt.wait_send()
 
 
-def assemble(g, fg_in, conv_f, sm_f, ag_s, ag_p, fg_out, conv_out, bias_out, proj_out, means_out, usage_out):
+def assemble(g, fg_in, conv_f, sm_f, ag, fg_out, conv_out, bias_out, proj_out, means_out, usage_out):
     nx, ny, zl_n, book, total = g["nx"], g["ny"], g["zl"], g["book"], g["total"]
     rs, rp, rpd, lanes = g["rs"], g["rp"], g["rpd"], g["chan"] // 128
     zl = lax.axis_index("tm")
@@ -472,12 +468,12 @@
     for cc in range(NC):
         for xx in range(nx):
             for level in range(2):
-                rows = [ag_s[cc, xx, yy].astype(F32)[level * rs:(level + 1) * rs] for yy in range(ny)]
+                rows = [ag[cc, xx, yy].astype(F32)[level * rs:(level + 1) * rs] for yy in range(ny)]
                 at = cc * per_c + xx * ny * rs
                 means_out[level, at:at + ny * rs, :] = jnp.concatenate(rows, 0).astype(BF)
             for yy in range(ny):
                 at = ((cc * nx + xx) * ny + yy) * rp
-                proj_out[at:at + rp, :] = ag_p[cc, yy, xx].astype(F32) * (1.0 / total)
+                proj_out[at:at + rp, :] = ag[cc, xx, yy].astype(F32)[2 * rs:] * (1.0 / total)
 
 
 def shards(g, feats, codes, conv_weight, conv_bias, proj_weight, codebooks):
@@ -548,17 +544,16 @@
     ]
     hbm = pl.BlockSpec(memory_space=pltpu.HBM)
     vmem = pl.BlockSpec(memory_space=pltpu.VMEM)
-    fg, conv_f, sm_f, ag_s, ag_p = pl.pallas_call(
+    fg, conv_f, sm_f, ag = pl.pallas_call(
         functools.partial(kernel, g),
         out_shape=(
             pltpu.VMEM((rows_in, chan), BF),
             pltpu.VMEM((tile, chan), F32),
             pltpu.VMEM((few, 128), F32),
-            pltpu.VMEM((NC, nx, ny, 2 * rs, dz), BF),
-            pltpu.VMEM((NC, ny, nx, rp, dz), BF),
+            pltpu.VMEM((NC, nx, ny, zrows, dz), BF),
         ),
         in_specs=[hbm] * 6,
-        out_specs=(vmem,) * 5,
+        out_specs=(vmem,) * 4,
         scratch_shapes=scratch,
         compiler_params=pltpu.CompilerParams(
             collective_id=0, has_side_effects=True, vmem_limit_bytes=32 << 20),
@@ -574,10 +569,10 @@
             jax.ShapeDtypeStruct((2, book // zln, dz), BF),
             jax.ShapeDtypeStruct((2, book // zln), F32),
         ),
-        in_specs=[vmem, vmem, vmem, vmem, vmem],
+        in_specs=[vmem] * 4,
         out_specs=(vmem, vmem, vmem, vmem, vmem, vmem),
         compiler_params=pltpu.CompilerParams(vmem_limit_bytes=8 << 20),
-    )(fg, conv_f, sm_f, ag_s, ag_p)
+    )(fg, conv_f, sm_f, ag)
     return fg, cg, bg.reshape(chan), pg, cm, cu
 
 

time: 57.4 us -> 55.1 us (0.960)
  Pallas kernels: 56.6 us -> 54.4 us
    pallas_call x1, Pallas kernels: 55.4 us -> 53.1 us  [shards(): pl.pallas_call(functools.partial(kernel, g), out_shape=(pltpu.VMEM((rows_...]
where the time goes in v4:
time: 55.1 us; the launch traced here: 55 us
  Pallas kernels  54.4 us (99%)
  between operations  0.64 us (1%)
    pallas_call x1, Pallas kernels, shards(): pl.pallas_call(functools.partial(kernel, g), out_shape=(pltpu.VMEM((rows_...  53.1 us
    pallas_call x1, Pallas kernels, shards(): pl.pallas_call(functools.partial(assemble, g), out_shape=(jax.ShapeDtypeS...  1.26 us

profile of v4, /device:TPU:1, one launch (start us, length us, event | category | flops | bytes accessed | tf_op | source)
XLA Modules:
  0.0 55.0 jit_solution(13402564622656701509)
XLA Ops:
  0.6 53.1 %shard_map.109 = (bf16[768,512]{1,0:T(8,128)(2,1)S(1)}, f32[16,512]{1,0:T(8,128)S(1)}, f32[8,128]{1,0:T(8,128)S(1)}, bf16[2,4,4,32,256]{4,3,2,1,0:T(8,128)(2,1)S(1)}) custom-call(bf16[768,512]{1,0:T(8,128)(2,1)} %feats.1, s32[1,2,384]{2,1,0:T(2,128)} %codes_in.1, bf16[2048,512]{1,0:T(8,128)(2,1)} %conv_w.1, f32[1,512]{1,0:T(1,128)} %bitcast.2, ...), custom_call_target="tpu_custom_call" | custom-call | tf_op jit(solution)/shard_map/pallas_call | solution.py:547
  53.7 1.3 %shard_map.110 = (bf16[768,512]{1,0:T(8,128)(2,1)}, f32[4,512]{1,0:T(4,128)}, f32[1,512]{1,0:T(1,128)}, f32[512,256]{1,0:T(8,128)}, bf16[2,256,256]{2,1,0:T(8,128)(2,1)}, /*index=5*/f32[2,256]{1,0:T(2,128)}) custom-call(bf16[768,512]{1,0:T(8,128)(2,1)S(1)} %get-tuple-element.16.fg_in, f32[16,512]{1,0:T(8,128)S(1)} %get-tuple-element.17.conv_f, ...), custom_call_target="tpu_custom_call" | custom-call | tf_op jit(solution)/shard_map/pallas_call | solution.py:562

commit v5 on v4

--- a/solution.py
+++ b/solution.py
@@ -376,14 +376,15 @@
             made = piece if made is None else made + piece
         return made
 
-    ca_y = stage2(ca_x, ca_1, ca_r1, ca_2, ca_r2, at_y, ny, y, x)
-    cb_x = stage2(cb_y, cb_1, cb_r1, cb_2, cb_r2, at_x, nx, x, y)
 
     told(2)
     zh_r[0] = summed(zl_c, zl_r, zl, zl_n).astype(BF)
     zh_c = sems.ring(zh_n, lambda d: zh_r.at[0], lambda d: zh_r.at[d], at_h)
     small(sm_ls, sm_l, zl, zl_n, sm_h.at[0])
     sm_hs = small_send(sm_h, at_h, zh_n)
+
+    ca_y = stage2(ca_x, ca_1, ca_r1, ca_2, ca_r2, at_y, ny, y, x)
+    cb_x = stage2(cb_y, cb_1, cb_r1, cb_2, cb_r2, at_x, nx, x, y)
 
     ca_d = finish(ca_y, ca_2, ca_r2, y)
     cb_d = finish(cb_x, cb_2, cb_r2, x)

time: 55.1 us -> 54.8 us (level)
  no operation moved by 1% of the time
where the time goes in v5:
time: 54.8 us; the launch traced here: 54.6 us
  Pallas kernels  54 us (99%)
  between operations  0.64 us (1%)
    pallas_call x1, Pallas kernels, shards(): pl.pallas_call(functools.partial(kernel, g), out_shape=(pltpu.VMEM((rows_...  52.7 us
    pallas_call x1, Pallas kernels, shards(): pl.pallas_call(functools.partial(assemble, g), out_shape=(jax.ShapeDtypeS...  1.26 us

profile of v5, /device:TPU:1, one launch (start us, length us, event | category | flops | bytes accessed | tf_op | source)
XLA Modules:
  0.0 54.6 jit_solution(2907752118215166298)
XLA Ops:
  0.6 52.7 %shard_map.109 = (bf16[768,512]{1,0:T(8,128)(2,1)S(1)}, f32[16,512]{1,0:T(8,128)S(1)}, f32[8,128]{1,0:T(8,128)S(1)}, bf16[2,4,4,32,256]{4,3,2,1,0:T(8,128)(2,1)S(1)}) custom-call(bf16[768,512]{1,0:T(8,128)(2,1)} %feats.1, s32[1,2,384]{2,1,0:T(2,128)} %codes_in.1, bf16[2048,512]{1,0:T(8,128)(2,1)} %conv_w.1, f32[1,512]{1,0:T(1,128)} %bitcast.2, ...), custom_call_target="tpu_custom_call" | custom-call | tf_op jit(solution)/shard_map/pallas_call | solution.py:548
  53.4 1.3 %shard_map.110 = (bf16[768,512]{1,0:T(8,128)(2,1)}, f32[4,512]{1,0:T(4,128)}, f32[1,512]{1,0:T(1,128)}, f32[512,256]{1,0:T(8,128)}, bf16[2,256,256]{2,1,0:T(8,128)(2,1)}, /*index=5*/f32[2,256]{1,0:T(2,128)}) custom-call(bf16[768,512]{1,0:T(8,128)(2,1)S(1)} %get-tuple-element.16.fg_in, f32[16,512]{1,0:T(8,128)S(1)} %get-tuple-element.17.conv_f, ...), custom_call_target="tpu_custom_call" | custom-call | tf_op jit(solution)/shard_map/pallas_call | solution.py:563
